TPU v7x, 32 devices: a whole 2x2x4 slice. The times are simulated.
32 devices in a mesh: shard: 16 (over z, y, x), replica: 2 (over core).
Axes of the slice: x: 2, y: 2, z: 4, core: 2. Of those that a mesh axis runs over, the one named last changes fastest.
Arguments:
- tokens: bfloat16 [32, 256, 768], P(('shard', 'replica')), may hold values from -6 to 6
- segment_ids: int32 [32, 256], P(('shard', 'replica')), may hold values from 0 to 7, never falling along the last dimension, each value on 1 to 128 neighbouring positions
- cotangent: bfloat16 [32, 256, 768], P(('shard', 'replica')), may hold values from -6 to 6
- w_qkv: float32 [768, 2304], P('shard'), may hold values from -5 to 5
- w_out: float32 [768, 768], P('shard'), may hold values from -0.625 to 0.625
- w_in: float32 [768, 3072], P('shard'), may hold values from -0.21875 to 0.21875
- w_down: float32 [3072, 768], P('shard'), may hold values from -0.109375 to 0.109375
- vectors: float32 [9984], P('shard'), may hold values from -1.5 to 1.5
- m_qkv: float32 [768, 2304], P('shard'), may hold values from -6 to 6
- m_out: float32 [768, 768], P('shard'), may hold values from -6 to 6
- m_in: float32 [768, 3072], P('shard'), may hold values from -6 to 6
- m_down: float32 [3072, 768], P('shard'), may hold values from -6 to 6
- m_vec: float32 [9984], P('shard'), may hold values from -6 to 6
- v_qkv: float32 [768, 2304], P('shard'), may hold values from 1 to 100
- v_out: float32 [768, 768], P('shard'), may hold values from 1 to 100
- v_in: float32 [768, 3072], P('shard'), may hold values from 1 to 100
- v_down: float32 [3072, 768], P('shard'), may hold values from 1 to 100
- v_vec: float32 [9984], P('shard'), may hold values from 1 to 100
Outputs:
- output: bfloat16 [32, 256, 768], P(('shard', 'replica'))
- input_grad: float32 [32, 256, 768], P(('shard', 'replica'))
- grad_qkv: float32 [768, 2304], P('shard')
- grad_out: float32 [768, 768], P('shard')
- grad_in: float32 [768, 3072], P('shard')
- grad_down: float32 [3072, 768], P('shard')
- grad_vec: float32 [9984], P('shard')
- new_qkv: float32 [768, 2304], P('shard')
- new_out: float32 [768, 768], P('shard')
- new_in: float32 [768, 3072], P('shard')
- new_down: float32 [3072, 768], P('shard')
- new_vec: float32 [9984], P('shard')
- new_m_qkv: float32 [768, 2304], P('shard')
- new_m_out: float32 [768, 768], P('shard')
- new_m_in: float32 [768, 3072], P('shard')
- new_m_down: float32 [3072, 768], P('shard')
- new_m_vec: float32 [9984], P('shard')
- new_v_qkv: float32 [768, 2304], P('shard')
- new_v_out: float32 [768, 768], P('shard')
- new_v_in: float32 [768, 3072], P('shard')
- new_v_down: float32 [3072, 768], P('shard')
- new_v_vec: float32 [9984], P('shard')
Inputs may be any that keep to these rules, and one draw needn't show every extreme that they name: `segment_ids`: segment ids never fall along a sequence; each document has 1 to 128 tokens.
All inputs are finite; a program needn't handle non-finite values.
Results may differ from a plain program's by a relative error of at most 0.014.
Values may be sent and summed in bfloat16 or wider, within the bound.
No kernel may reach another device: no remote copies, remote signals or barrier semaphores. Data moves between devices by JAX's collectives and lax.ppermute only.
A program may use at most 128 MiB of HBM per device.

v0:
```python
import functools

import jax
import jax.numpy as jnp
import numpy as np
from jax import lax
from jax.experimental import pallas as pl
from jax.experimental.pallas import tpu as pltpu
from jax.sharding import PartitionSpec as P

D = 768
HEADS = 12
HEAD_DIM = 64
FF = 3072
ROT = 16
STEP = 5


norm_eps = 1e-05
learn_rate = 0.01
beta_first = 0.9
beta_second = 0.999
adam_eps = 1e-08
decay_rate = 0.1


def split_vectors(vectors):
    bounds = [0, D, 2 * D, 3 * D, 4 * D, 7 * D, 8 * D, 8 * D + FF, 9 * D + FF]
    return [vectors[bounds[number] : bounds[number + 1]] for number in range(8)]


def rotary_lanes(length, heads):
    half_rot = ROT // 2
    freqs = 10000.0 ** (-np.arange(half_rot) * 2.0 / ROT)
    angles = np.arange(length)[:, None] * freqs[None, :]
    cosine = np.ones((length, HEAD_DIM))
    sine = np.zeros((length, HEAD_DIM))
    cosine[:, :ROT] = np.tile(np.cos(angles), (1, 2))
    sine[:, :ROT] = np.tile(np.sin(angles), (1, 2))
    partner = np.zeros((HEAD_DIM, HEAD_DIM))
    for lane in range(half_rot):
        partner[lane + half_rot, lane] = -1.0
        partner[lane, lane + half_rot] = 1.0
    cosine = jnp.tile(jnp.asarray(cosine, jnp.float32), (1, heads))
    sine = jnp.tile(jnp.asarray(sine, jnp.float32), (1, heads))
    return cosine, sine, jnp.asarray(np.kron(np.eye(heads), partner), jnp.bfloat16)


def contract(left, right, left_dim, right_dim):
    return lax.dot_general(
        left, right, (((left_dim,), (right_dim,)), ((), ())), preferred_element_type=jnp.float32
    )


def attention_kernel(
    ways,
    heads,
    normed_ref,
    cot_ref,
    seg_col_ref,
    seg_row_ref,
    qkv_ref,
    out_ref,
    bias_ref,
    cos_ref,
    sin_ref,
    partner_ref,
    mixed_ref,
    branch_ref,
    slope_ref,
    sums_ref,
    grad_qkv_ref,
    grad_out_ref,
    qkv_total,
    out_total,
):
    half = jnp.bfloat16
    wide = jnp.float32
    step = pl.program_id(0)
    cols = heads * HEAD_DIM
    cosine, sine, partner = cos_ref[...], sin_ref[...], partner_ref[...]

    def partners(values):
        high = values.astype(half)
        low = (values - high.astype(wide)).astype(half)
        return contract(high, partner, 1, 0) + contract(low, partner, 1, 0)

    normed = normed_ref[...]
    cot = cot_ref[...]
    projected = contract(normed, qkv_ref[...], 1, 0) + bias_ref[...]
    query, keyed = projected[:, :cols], projected[:, cols : 2 * cols]
    query = (query * cosine + partners(query) * sine).astype(half)
    keyed = (keyed * cosine + partners(keyed) * sine).astype(half)
    valued = projected[:, 2 * cols : 3 * cols].astype(half)
    grad_mixed = contract(cot, out_ref[...], 1, 1).astype(half)
    length = normed.shape[0]
    row = lax.broadcasted_iota(jnp.int32, (length, length), 0)
    column = lax.broadcasted_iota(jnp.int32, (length, length), 1)
    allowed = (seg_col_ref[0] == seg_row_ref[0]) & (row >= column)
    mixed, grad_q, grad_k, grad_v = [], [], [], []
    for head in range(heads):
        lanes = slice(head * HEAD_DIM, (head + 1) * HEAD_DIM)
        q, k, v, g = query[:, lanes], keyed[:, lanes], valued[:, lanes], grad_mixed[:, lanes]
        scores = jnp.where(allowed, contract(q, k, 1, 1) * HEAD_DIM ** (-0.5), -1e30)
        shifted = jnp.exp(scores - jnp.max(scores, axis=1, keepdims=True))
        probs_full = shifted / jnp.sum(shifted, axis=1, keepdims=True)
        probs = probs_full.astype(half)
        mixed.append(contract(probs, v, 1, 0))
        grad_v.append(contract(probs, g, 0, 0))
        grad_probs = contract(g, v, 1, 1)
        inner = jnp.sum(probs_full * grad_probs, axis=1, keepdims=True)
        grad_scores = (probs_full * (grad_probs - inner) * HEAD_DIM ** (-0.5)).astype(half)
        grad_q.append(contract(grad_scores, k, 1, 0))
        grad_k.append(contract(grad_scores, q, 0, 0))
    mixed = jnp.concatenate(mixed, axis=1).astype(half)
    grad_q = jnp.concatenate(grad_q, axis=1)
    grad_k = jnp.concatenate(grad_k, axis=1)
    grad_v = jnp.concatenate(grad_v, axis=1)
    grad_q = grad_q * cosine - partners(grad_q) * sine
    grad_k = grad_k * cosine - partners(grad_k) * sine
    grad_projected = jnp.concatenate([grad_q, grad_k, grad_v, jnp.zeros_like(grad_v)], axis=1)
    projected_half = grad_projected.astype(half)
    sums_ref[0] = jnp.sum(grad_projected, axis=0, keepdims=True)
    mixed_ref[...] = mixed
    branch_ref[...] = contract(mixed, out_ref[...], 1, 0)
    slope_ref[...] = contract(projected_half, qkv_ref[...], 1, 1)

    @pl.when(step == 0)
    def _():
        qkv_total[...] = jnp.zeros_like(qkv_total)
        out_total[...] = jnp.zeros_like(out_total)

    qkv_total[...] += contract(normed, projected_half, 0, 0)
    out_total[...] += contract(mixed, cot, 0, 0)

    @pl.when(step == pl.num_programs(0) - 1)
    def _():
        grad_qkv_ref[...] = qkv_total[...].astype(half)
        for way in range(ways):
            grad_out_ref[way] = out_total[:, way * cols : (way + 1) * cols].astype(half)


def attention(normed, cot, seg, qkv_all, out_all, bias, ways, heads):
    half = jnp.bfloat16
    wide = jnp.float32
    seqs, length = seg.shape
    count = seqs * length
    cols = heads * HEAD_DIM
    width = qkv_all.shape[1]
    cosine, sine, partner = rotary_lanes(length, heads)
    bias_row = jnp.pad(bias, (0, width - 3 * cols))[None]

    def block(rows, lanes):
        return pl.BlockSpec((rows, lanes), lambda s: (s, 0))

    def whole(*shape):
        return pl.BlockSpec(shape, lambda s: (0,) * len(shape))

    flops = 2 * count * (2 * D * width * 2 + 3 * D * cols + 7 * length * cols)
    return pl.pallas_call(
        functools.partial(attention_kernel, ways, heads),
        grid=(seqs,),
        in_specs=[
            block(length, D),
            block(length, D),
            pl.BlockSpec((1, length, 1), lambda s: (s, 0, 0)),
            pl.BlockSpec((1, 1, length), lambda s: (s, 0, 0)),
            whole(D, width),
            whole(cols, D),
            whole(1, width),
            whole(length, cols),
            whole(length, cols),
            whole(cols, cols),
        ],
        out_specs=[
            block(length, cols),
            block(length, D),
            block(length, D),
            pl.BlockSpec((1, 1, width), lambda s: (s, 0, 0)),
            whole(D, width),
            whole(ways, cols, cols),
        ],
        out_shape=[
            jax.ShapeDtypeStruct((count, cols), half),
            jax.ShapeDtypeStruct((count, D), wide),
            jax.ShapeDtypeStruct((count, D), wide),
            jax.ShapeDtypeStruct((seqs, 1, width), wide),
            jax.ShapeDtypeStruct((D, width), half),
            jax.ShapeDtypeStruct((ways, cols, cols), half),
        ],
        scratch_shapes=[pltpu.VMEM((D, width), wide), pltpu.VMEM((cols, D), wide)],
        compiler_params=pltpu.CompilerParams(dimension_semantics=("arbitrary",)),
        cost_estimate=pl.CostEstimate(
            flops=flops, bytes_accessed=18 * 1024 * 1024, transcendentals=seqs * heads * length**2
        ),
        name="attention_block",
    )(
        normed,
        cot,
        seg[:, :, None],
        seg[:, None, :],
        qkv_all,
        out_all,
        bias_row,
        cosine,
        sine,
        partner,
    )


class Group:
    def __init__(self, mesh):
        self.shards = mesh.shape["shard"]
        self.replicas = mesh.shape["replica"]
        self.rings = self.shards <= 16 and self.shards % 4 == 0
        self.twins = 2 if self.rings and HEADS % (2 * self.replicas) == 0 else 1
        self.ways = self.twins * self.replicas
        self.groups = self.shards // self.twins
        self.pairs = 2 if self.groups % 2 == 0 else 1
        self.lines = self.groups // self.pairs

    def place(self):
        shard = lax.axis_index("shard")
        self.twin = shard % self.twins
        self.group = shard // self.twins
        self.pair = self.group % self.pairs
        self.line = self.group // self.pairs
        self.replica = lax.axis_index("replica")
        self.rank = self.twin * self.replicas + self.replica


    def from_twin(self, array):
        return lax.ppermute(array, "shard", [(s, s ^ 1) for s in range(self.shards)])

    def from_pair(self, array):
        step = self.twins
        return lax.ppermute(array, "shard", [(s, s ^ step) for s in range(self.shards)])

    def along_line(self, array, hops):
        block = self.twins * self.pairs
        return lax.ppermute(
            array,
            "shard",
            [
                (s, ((s // block + hops) % self.lines) * block + s % block)
                for s in range(self.shards)
            ],
        )

    def to_replica(self, array, hops):
        size = self.replicas
        return lax.ppermute(array, "replica", [(c, (c + hops) % size) for c in range(size)])

    def twins_in_order(self, own, far):
        return jnp.stack(
            [jnp.where(self.twin == 0, own, far), jnp.where(self.twin == 0, far, own)]
        )

    def to_rank(self, array, twin_flip, hops):
        size = self.replicas
        pairs = [
            (s * size + c, (s ^ twin_flip) * size + (c + hops) % size)
            for s in range(self.shards)
            for c in range(size)
        ]
        return lax.ppermute(array, ("shard", "replica"), pairs)


    def gather_whole(self, piece):
        members = None
        if self.twins > 1:
            members = [
                [group * self.twins + twin for group in range(self.groups)]
                for twin in range(self.twins)
            ]
        return lax.all_gather(piece, "shard", axis=0, tiled=False, axis_index_groups=members)

    def gather(self, piece):
        if not self.rings:
            return self.gather_whole(piece)
        held = [piece]
        for hops in range(1, self.lines):
            held.append(self.along_line(piece, hops))
        buffer = jnp.zeros((self.groups,) + piece.shape, piece.dtype)
        zeros = (0,) * piece.ndim
        for hops, block in enumerate(held):
            line = (self.line - hops) % self.lines
            own = line * self.pairs + self.pair
            buffer = lax.dynamic_update_slice(buffer, block[None], (own,) + zeros)
        for hops, block in enumerate(held):
            line = (self.line - hops) % self.lines
            other = line * self.pairs + (self.pair ^ 1)
            buffer = lax.dynamic_update_slice(
                buffer, self.from_pair(block)[None], (other,) + zeros
            )
        return buffer

    def scatter(self, terms, pieces=1, marks=None, before=()):
        wide = jnp.float32
        if not self.rings:
            total = lax.psum_scatter(terms.astype(wide), "shard", scatter_dimension=0, tiled=False)
            return total
        halves = terms.reshape((self.lines, self.pairs) + terms.shape[1:])
        keep = lax.dynamic_index_in_dim(halves, self.pair, 1, keepdims=False)
        give = lax.dynamic_index_in_dim(halves, self.pair ^ 1, 1, keepdims=False)

        def block(array, hops):
            return lax.dynamic_index_in_dim(
                array, (self.line + hops) % self.lines, 0, keepdims=False
            )

        order = [hops for hops in range(1, self.lines)] + [0]
        if pieces == 1:
            merged = keep.astype(wide) + self.from_pair(give).astype(wide)
            if before:
                merged = after(merged, *before)
            if marks is not None:
                marks.append(merged)
            sums = {hops: block(merged, hops) for hops in order}
        else:
            sums = {}
            size = -(-self.lines // pieces)
            for start in range(0, self.lines, size):
                chosen = order[start : start + size]
                far = self.from_pair(jnp.stack([block(give, hops) for hops in chosen]))
                if before:
                    far = after(far, *before)
                for place, hops in enumerate(chosen):
                    sums[hops] = block(keep, hops).astype(wide) + far[place].astype(wide)
        total = sums[0]
        for hops in range(1, self.lines):
            total = total + self.along_line(sums[hops].astype(jnp.bfloat16), hops).astype(wide)
        return total

    def gather_sequences(self, array):
        across = array[None]
        if self.twins == 2:
            across = jnp.stack([array, self.from_twin(array)])
        slots = [across]
        for hops in range(1, self.replicas):
            slots.append(self.to_replica(across, self.replicas - hops))
        return jnp.stack(slots).reshape((-1,) + array.shape[1:])

    def reduce_sequences(self, partial, marks=None):
        wire = jnp.bfloat16
        wide = jnp.float32
        shape = partial.shape
        batch = shape[0] // self.ways
        slots = partial.reshape((self.replicas, self.twins, batch) + shape[1:])
        total = slots[0]
        for hops in range(1, self.replicas):
            total = total + self.to_replica(slots[hops].astype(wire), hops).astype(wide)
        own = total[0]
        if self.twins == 2:
            give = total[1].astype(wire)
            if marks is not None:
                marks.append(give)
            own = own + self.from_twin(give).astype(wide)
        return own


    def share(self, pick):
        own = pick(self.rank)
        if self.twins == 1:
            return own[None]
        far = self.from_twin(pick((self.twin ^ 1) * self.replicas + self.replica))
        return self.twins_in_order(own, far)

    def from_replicas(self, own):
        held = [own] + [self.to_replica(own, hops) for hops in range(1, self.replicas)]
        if self.replicas == 2:
            return jnp.stack(
                [
                    jnp.where(self.replica == 0, held[0], held[1]),
                    jnp.where(self.replica == 0, held[1], held[0]),
                ]
            )
        result = jnp.zeros((self.replicas,) + own.shape, own.dtype)
        for hops, part in enumerate(held):
            source = (self.replica - hops) % self.replicas
            result = lax.dynamic_update_slice(result, part[None], (source,) + (0,) * own.ndim)
        return result

    def unshare(self, rows):
        half = jnp.bfloat16
        own = lax.dynamic_index_in_dim(rows, self.twin, 0, keepdims=False).astype(half)
        if self.twins == 2:
            give = lax.dynamic_index_in_dim(rows, self.twin ^ 1, 0, keepdims=False)
            both = self.twins_in_order(own, self.from_twin(give.astype(half)))
        else:
            both = own[None]
        stacked = jnp.swapaxes(self.from_replicas(both), 0, 1)
        return stacked.reshape((self.ways,) + own.shape)

    def routes(self):
        pairs = []
        for holder in range(self.shards * self.replicas):
            rank, group = holder // self.groups, holder % self.groups
            shard = group * self.twins + rank // self.replicas
            pairs.append((holder, shard * self.replicas + rank % self.replicas))
        return pairs

    def to_users(self, piece):
        return lax.ppermute(piece, ("shard", "replica"), self.routes())

    def to_holders(self, piece):
        back = [(user, holder) for holder, user in self.routes()]
        return lax.ppermute(piece, ("shard", "replica"), back)


def after(value, *earlier):
    return lax.optimization_barrier((value, *earlier))[0]


def adamw(weight, gradient, moment_one, moment_two, decay_on):
    moment_one = beta_first * moment_one + (1.0 - beta_first) * gradient
    moment_two = beta_second * moment_two + (1.0 - beta_second) * gradient * gradient
    first_hat = moment_one / (1.0 - beta_first**STEP)
    second_hat = moment_two / (1.0 - beta_second**STEP)
    updated = weight - learn_rate * (
        first_hat / (jnp.sqrt(second_hat) + adam_eps) + decay_on * weight
    )
    return (updated, moment_one, moment_two)


def step(
    group,
    tokens,
    segment_ids,
    cotangent,
    w_qkv,
    w_out,
    w_in,
    w_down,
    vectors,
    m_qkv,
    m_out,
    m_in,
    m_down,
    m_vec,
    v_qkv,
    v_out,
    v_in,
    v_down,
    v_vec,
):
    group.place()
    half = jnp.bfloat16
    wide = jnp.float32
    ways = group.ways
    groups = group.groups
    twins = group.twins
    heads = HEADS // ways
    rows = w_qkv.shape[0]
    units = FF // (groups * ways)
    out_cols = D // ways
    width = 4 * out_cols
    batch, length = tokens.shape[:2]
    seqs = batch * ways
    count = seqs * length
    vec_size = vectors.shape[0]
    vec_rows = -(-vec_size // (8 * width)) * 8

    qkv_half = w_qkv.astype(half).reshape(rows, 3, ways, out_cols)
    in_half = w_in.astype(half).reshape(rows, groups, ways, units)
    down_half = w_down.astype(half).reshape(group.replicas, units, D)
    vec_half = jnp.pad(vectors.astype(half), (0, vec_rows * width - vec_size))
    vec_half = vec_half.reshape(vec_rows, width)
    out_rows = rows // group.replicas
    out_half = lax.dynamic_slice_in_dim(w_out, group.replica * out_rows, out_rows, 0)
    out_piece = group.to_users(out_half.astype(half))
    out_piece = out_piece.reshape(out_rows, ways, out_cols).transpose(1, 0, 2)

    def pick(rank):
        qkv = lax.dynamic_index_in_dim(qkv_half, rank, 2, keepdims=False).reshape(rows, -1)
        qkv = jnp.concatenate([qkv, jnp.zeros((rows, out_cols), half)], axis=1)
        into = lax.dynamic_index_in_dim(in_half, rank, 2, keepdims=False).reshape(rows, -1)
        return jnp.concatenate([qkv, vec_half, into], axis=0)

    shared = group.share(pick)
    down_piece = lax.dynamic_index_in_dim(down_half, group.replica, 0, keepdims=False)
    second_piece = jnp.concatenate(
        [shared[:, rows + vec_rows :].reshape(-1, width), down_piece.reshape(-1, width)], axis=0
    )
    second = group.gather_whole(second_piece)
    first_piece = lax.dynamic_update_slice(
        shared[:, : rows + vec_rows],
        out_piece.reshape(twins, rows, out_cols),
        (0, 0, 3 * out_cols),
    )

    seg_rows = jnp.pad(segment_ids.astype(half)[:, None], ((0, 0), (0, 7), (0, D - length)))
    pack = jnp.concatenate([tokens, cotangent, seg_rows], axis=1)
    packs = group.gather_sequences(after(pack, shared))
    x_seqs = packs[:, :length]
    cot = packs[:, length : 2 * length]
    seg = packs[:, 2 * length, :length].astype(wide)

    first = group.gather(first_piece)
    qkv_all = first[:, :, :rows].reshape(D, width)
    vec_all = first[:, :, rows:].reshape(group.shards, -1)[:, :vec_size].reshape(-1).astype(wide)
    in_all = second[:, : twins * rows].reshape(D, width)
    down_all = second[:, twins * rows :].reshape(width, D)
    out_all = first[:, :, :rows, 3 * out_cols :].reshape(groups, ways, out_rows, out_cols)
    out_all = out_all.transpose(0, 2, 1, 3).reshape(out_cols, D)

    gain_one, offset_one, gain_two, offset_two, bias_qkv, bias_out, bias_in, bias_down = (
        split_vectors(vec_all)
    )
    bias_qkv_own = lax.dynamic_index_in_dim(
        bias_qkv.reshape(3, ways, -1), group.rank, 1, keepdims=False
    ).reshape(-1)
    bias_in_own = lax.dynamic_index_in_dim(
        bias_in.reshape(groups, ways, units), group.rank, 1, keepdims=False
    ).reshape(-1)

    inputs = x_seqs.reshape(count, D).astype(wide)
    center = inputs - jnp.mean(inputs, axis=-1, keepdims=True)
    spread = jnp.mean(center * center, axis=-1, keepdims=True)
    unit = center * lax.rsqrt(spread + norm_eps)
    normed_attn = (unit * gain_one + offset_one).astype(half)
    normed_mlp = (unit * gain_two + offset_two).astype(half)
    cot_flat = cot.reshape(count, D)
    _, branch_attn, partial_attn, sums_attn, grad_qkv, grad_out = attention(
        normed_attn, cot_flat, seg, qkv_all, out_all, bias_qkv_own, ways, heads
    )
    bias_qkv_grad = jnp.sum(sums_attn, axis=(0, 1))[: 3 * out_cols]
    out_back = grad_out.reshape(ways, groups, out_rows, out_cols).transpose(1, 0, 2, 3)
    first_grad = jnp.concatenate(
        [
            grad_qkv[:, : 3 * out_cols].reshape(groups, twins * rows, -1),
            out_back.reshape(groups, twins * rows, out_cols),
        ],
        axis=2,
    )
    marks = []
    first_sum = group.scatter(first_grad, 1, marks)
    first_total = group.unshare(first_sum[:, : 3 * out_cols].reshape(twins, rows, -1))
    out_sum = first_sum[:, 3 * out_cols :].astype(half).reshape(ways, out_rows, out_cols)
    out_sum = out_sum.transpose(1, 0, 2).reshape(out_rows, D)
    out_total = group.from_replicas(group.to_holders(out_sum)).reshape(rows, D)

    hidden = jnp.dot(normed_mlp, in_all, preferred_element_type=wide) + bias_in_own
    share_below = 0.5 + 0.5 * lax.erf(hidden * 0.5**0.5)
    act_half = (hidden * share_below).astype(half)
    grad_down = lax.dot_general(
        act_half, cot_flat, (((0,), (0,)), ((), ())), preferred_element_type=wide
    ).astype(half)
    sent = []
    grad_act = lax.dot_general(
        after(cot_flat, grad_down, *marks), down_all, (((1,), (1,)), ((), ())), preferred_element_type=wide
    )
    density = jnp.exp(-0.5 * hidden * hidden) * (2.0 * np.pi) ** -0.5
    grad_hidden = grad_act * (share_below + hidden * density)
    hidden_half = grad_hidden.astype(half)
    grad_in = lax.dot_general(
        normed_mlp, hidden_half, (((0,), (0,)), ((), ())), preferred_element_type=wide
    ).astype(half)
    partial_mlp = lax.dot_general(
        hidden_half, in_all, (((1,), (1,)), ((), ())), preferred_element_type=wide
    )
    partial_out = branch_attn + jnp.dot(act_half, down_all, preferred_element_type=wide)
    branch = group.reduce_sequences(partial_out.reshape(seqs, length, D), sent)
    output = (tokens.astype(wide) + branch + (bias_out + bias_down)).astype(half)

    partial_slope = partial_attn * gain_one + partial_mlp * gain_two
    own = batch * length
    own_unit = unit[:own]
    own_cot = cotangent.reshape(own, D).astype(wide)
    slope = group.reduce_sequences(partial_slope.reshape(seqs, length, D), sent).reshape(own, D)
    down_total = group.from_replicas(
        group.scatter(grad_down.reshape(groups, units, D), before=sent[:1]).astype(half)
    )
    scale = lax.rsqrt(spread[:own] + norm_eps)
    back = scale * (
        slope
        - jnp.mean(slope, axis=-1, keepdims=True)
        - own_unit * jnp.mean(slope * own_unit, axis=-1, keepdims=True)
    )
    input_grad = (own_cot + back).reshape(batch, length, D)

    def columns(values, outer):
        zero = jnp.zeros((outer, ways, values.shape[0] // outer), wide)
        return lax.dynamic_update_slice(
            zero, values.reshape(outer, 1, -1), (0, group.rank, 0)
        ).reshape(-1)

    column_sum = jnp.sum(own_cot, axis=0)
    vector_grad = jnp.concatenate(
        [
            jnp.sum(partial_attn * unit, axis=0),
            jnp.sum(partial_attn, axis=0),
            jnp.sum(partial_mlp * unit, axis=0),
            jnp.sum(partial_mlp, axis=0),
            columns(bias_qkv_grad, 3),
            column_sum,
            columns(jnp.sum(grad_hidden, axis=0), groups),
            column_sum,
        ]
    ).reshape(groups, twins, vec_size)
    vector_grad = jnp.pad(
        vector_grad.astype(half), ((0, 0), (0, 0), (0, vec_rows * width - vec_size))
    ).reshape(groups, twins, vec_rows, width)
    in_grad = jnp.concatenate([grad_in.reshape(groups, twins, rows, width), vector_grad], axis=2)
    in_total = group.unshare(group.scatter(in_grad, 2, before=sent))
    vec_total = jnp.sum(in_total[:, rows:].astype(wide), axis=0).reshape(-1)[:vec_size]

    totals = (
        first_total.reshape(ways, rows, 3, out_cols)
        .transpose(1, 2, 0, 3)
        .reshape(rows, -1)
        .astype(wide),
        out_total.astype(wide),
        in_total[:, :rows]
        .reshape(ways, rows, groups, units)
        .transpose(1, 2, 0, 3)
        .reshape(rows, -1)
        .astype(wide),
        down_total.reshape(-1, D).astype(wide),
        vec_total,
    )
    masters = (w_qkv, w_out, w_in, w_down, vectors)
    firsts = (m_qkv, m_out, m_in, m_down, m_vec)
    seconds = (v_qkv, v_out, v_in, v_down, v_vec)
    decays = (decay_rate, decay_rate, decay_rate, decay_rate, 0.0)
    results = [
        adamw(masters[number], totals[number], firsts[number], seconds[number], decays[number])
        for number in range(5)
    ]
    return (
        output,
        input_grad,
        *totals,
        *(result[0] for result in results),
        *(result[1] for result in results),
        *(result[2] for result in results),
    )


def solution(mesh):
    placed = (
        P(("shard", "replica"), None, None),
        P(("shard", "replica"), None),
        P(("shard", "replica"), None, None),
        P("shard", None),
        P("shard", None),
        P("shard", None),
        P("shard", None),
        P("shard"),
        P("shard", None),
        P("shard", None),
        P("shard", None),
        P("shard", None),
        P("shard"),
        P("shard", None),
        P("shard", None),
        P("shard", None),
        P("shard", None),
        P("shard"),
    )
    return jax.shard_map(
        functools.partial(step, Group(mesh)),
        mesh=mesh,
        in_specs=placed,
        out_specs=(
            P(("shard", "replica"), None, None),
            P(("shard", "replica"), None, None),
            P("shard", None),
            P("shard", None),
            P("shard", None),
            P("shard", None),
            P("shard"),
            P("shard", None),
            P("shard", None),
            P("shard", None),
            P("shard", None),
            P("shard"),
            P("shard", None),
            P("shard", None),
            P("shard", None),
            P("shard", None),
            P("shard"),
            P("shard", None),
            P("shard", None),
            P("shard", None),
            P("shard", None),
            P("shard"),
        ),
        check_vma=False,
    )
```

profile of v0, /device:TPU:0, one launch (start us, length us, event | category | flops | bytes accessed | tf_op | source)
XLA Modules:
  0.0 247.5 jit_solution(16223981538474396485)
XLA Ops:
  12.5 3.0 %collective-permute-start = (bf16[104,768]{1,0:T(8,128)(2,1)S(1)}, bf16[104,768]{1,0:T(8,128)(2,1)S(1)}, u32[]{:S(2)}, u32[]{:S(2)}) collective-permute-start(bf16[104,768]{1,0:T(8,128)(2,1)S(1)} %fusion.57), channel_id=1, source_target_pairs={{0,2},{2,0},{4,6},{6,4},{8,10},{10,8},{12,14},{14,12},{16,18},{18,... | collective-permute-start | bytes 479240 | tf_op jit(solution)/shard_map/ppermute | solution.py:233
  16.3 4.3 %collective-permute-start.1 = (bf16[1,520,768]{2,1,0:T(8,128)(2,1)S(1)}, bf16[1,520,768]{2,1,0:T(8,128)(2,1)S(1)}, u32[]{:S(2)}, u32[]{:S(2)}) collective-permute-start(bf16[1,520,768]{2,1,0:T(8,128)(2,1)S(1)} %fusion.7), channel_id=1, source_target_pairs={{0,2},{2,0},{4,6},{6,4},{8,10},{10,8},{12,14},{14,12},{16,18},{18,... | collective-permute-start | bytes 2396168 | tf_op jit(solution)/shard_map/ppermute | solution.py:233
  25.7 5.2 %collective-permute-start.5 = (bf16[2,56,768]{2,1,0:T(8,128)(2,1)S(1)}, bf16[2,56,768]{2,1,0:T(8,128)(2,1)S(1)}, u32[]{:S(2)}, u32[]{:S(2)}) collective-permute-start(bf16[2,56,768]{2,1,0:T(8,128)(2,1)S(1)} %dynamic_update_slice.33), channel_id=1, source_target_pairs={{0,16},{2,18},{4,20},{6,22},{8,24},{10,26},{12,28},{14,30},{16,0},... | collective-permute-start | bytes 516104 | tf_op jit(solution)/shard_map/ppermute | solution.py:241
  32.9 2.8 %collective-permute-done.4 = bf16[2,56,768]{2,1,0:T(8,128)(2,1)} collective-permute-done((bf16[2,56,768]{2,1,0:T(8,128)(2,1)S(1)}, bf16[2,56,768]{2,1,0:T(8,128)(2,1)}, u32[]{:S(2)}, u32[]{:S(2)}) %collective-permute-start.4) | collective-permute-done | bytes 172064 | tf_op jit(solution)/shard_map/ppermute | solution.py:241
  37.4 3.6 %collective-permute-done.5 = bf16[2,56,768]{2,1,0:T(8,128)(2,1)S(1)} collective-permute-done((bf16[2,56,768]{2,1,0:T(8,128)(2,1)S(1)}, bf16[2,56,768]{2,1,0:T(8,128)(2,1)S(1)}, u32[]{:S(2)}, u32[]{:S(2)}) %collective-permute-start.5) | collective-permute-done | bytes 172064 | tf_op jit(solution)/shard_map/ppermute | solution.py:241
  41.0 2.6 %collective-permute-start.9 = (bf16[2,56,768]{2,1,0:T(8,128)(2,1)S(1)}, bf16[2,56,768]{2,1,0:T(8,128)(2,1)S(1)}, u32[]{:S(2)}, u32[]{:S(2)}) collective-permute-start(bf16[2,56,768]{2,1,0:T(8,128)(2,1)S(1)} %collective-permute-done.5), channel_id=1, source_target_pairs={{0,4},{2,6},{4,0},{6,2},{8,12},{10,14},{12,8},{14,10},{16,20},{18,... | collective-permute-start | bytes 516104 | tf_op jit(solution)/shard_map/ppermute | solution.py:237
  45.5 2.5 %fusion.79 = (bf16[1,2,1,520,768]{4,3,1,2,0:T(8,128)(2,1)}, bf16[2,1,520,768]{3,2,1,0:T(8,128)(2,1)S(1)}) fusion(bf16[1,1,520,768]{3,2,1,0:T(8,128)(2,1)} %bitcast.311, bf16[1,1,520,768]{3,2,1,0:T(8,128)(2,1)S(1)} %bitcast.293), kind=kLoop, calls=%fused_computation.226 | loop fusion | flops 798720 | bytes 4792320 | tf_op jit(solution)/shard_map/stack | solution.py:342
  49.4 2.9 %collective-permute-done.10 = bf16[2,56,768]{2,1,0:T(8,128)(2,1)S(1)} collective-permute-done((bf16[2,56,768]{2,1,0:T(8,128)(2,1)S(1)}, bf16[2,56,768]{2,1,0:T(8,128)(2,1)S(1)}, u32[]{:S(2)}, u32[]{:S(2)}) %collective-permute-start.10) | collective-permute-done | bytes 172064 | tf_op jit(solution)/shard_map/ppermute | solution.py:237
  55.9 2.2 pad_maximum_fusion
  63.7 22.4 %attention_block.1 = (bf16[1024,192]{1,0:T(8,128)(2,1)}, f32[1024,768]{1,0:T(8,128)}, f32[1024,768]{1,0:T(8,128)}, f32[4,1,768]{2,1,0:T(1,128)}, bf16[768,768]{1,0:T(8,128)(2,1)}, /*index=5*/bf16[4,192,192]{2,1,0:T(8,128)(2,1)}) custom-call(bf16[1024,768]{1,0:T(8,128)(2,1)} %add_convert_fusion.2.normed_ref, bf16[1024,768]{1,0:T(8,128)(2,1)} %bitcast.297, ...), custom_call_target="tpu_custom_call" | custom-call | flops 6442450944 | bytes 18874368 | tf_op jit(solution)/shard_map/attention_block/pallas_call | solution.py:160
  92.5 11.9 %collective-permute-done.13 = bf16[4,96,768]{2,1,0:T(8,128)(2,1)} collective-permute-done((bf16[4,96,768]{2,1,0:T(8,128)(2,1)}, bf16[4,96,768]{2,1,0:T(8,128)(2,1)}, u32[]{:S(2)}, u32[]{:S(2)}) %collective-permute-start.13) | collective-permute-done | bytes 589856 | tf_op jit(solution)/shard_map/ppermute | solution.py:237
  105.9 4.4 %collective-permute-start.18 = (bf16[96,768]{1,0:T(8,128)(2,1)S(1)}, bf16[96,768]{1,0:T(8,128)(2,1)S(1)}, u32[]{:S(2)}, u32[]{:S(2)}) collective-permute-start(bf16[96,768]{1,0:T(8,128)(2,1)S(1)} %get-tuple-element.88), channel_id=1, source_target_pairs={{0,24},{2,26},{4,28},{6,30},{8,0},{10,2},{12,4},{14,6},{16,8},{18,... | collective-permute-start | bytes 442376 | tf_op jit(solution)/shard_map/ppermute | solution.py:241
  110.3 4.8 %collective-permute-start.17 = (bf16[96,768]{1,0:T(8,128)(2,1)S(1)}, bf16[96,768]{1,0:T(8,128)(2,1)S(1)}, u32[]{:S(2)}, u32[]{:S(2)}) collective-permute-start(bf16[96,768]{1,0:T(8,128)(2,1)S(1)} %get-tuple-element.89), channel_id=1, source_target_pairs={{0,16},{2,18},{4,20},{6,22},{8,24},{10,26},{12,28},{14,30},{16,0},... | collective-permute-start | bytes 442376 | tf_op jit(solution)/shard_map/ppermute | solution.py:241
  117.2 10.7 %collective-permute-done.17 = bf16[96,768]{1,0:T(8,128)(2,1)S(1)} collective-permute-done((bf16[96,768]{1,0:T(8,128)(2,1)S(1)}, bf16[96,768]{1,0:T(8,128)(2,1)S(1)}, u32[]{:S(2)}, u32[]{:S(2)}) %collective-permute-start.17) | collective-permute-done | bytes 147488 | tf_op jit(solution)/shard_map/ppermute | solution.py:241
  137.6 2.2 reshape.463
  139.8 2.3 copy.82
  144.4 2.7 %multiply_subtract_fusion.2 = (f32[48,2304]{1,0:T(8,128)}, f32[48,2304]{1,0:T(8,128)}, f32[48,2304]{1,0:T(8,128)}) fusion(f32[48,2304]{1,0:T(8,128)} %param.24, f32[48,2304]{1,0:T(8,128)} %reshape.450, f32[48,2304]{1,0:T(8,128)} %param.29, f32[48,2304]{1,0:T(8,128)} %param.34), kind=kLoop, calls=%fused_computation.87 | loop fusion | flops 1658880 | bytes 3096576 | tf_op jit(solution)/shard_map/sub | solution.py:420
  149.1 4.0 %multiply_convert_fusion = (bf16[1024,768]{1,0:T(8,128)(2,1)S(1)}, f32[1024,768]{1,0:T(8,128)S(1)}) fusion(f32[768]{0:T(1024)S(1)} %copy-done.30, bf16[1024,768]{1,0:T(8,128)(2,1)S(1)} %bitcast.300, bf16[768,768]{1,0:T(8,128)(2,1)S(1)} %bitcast.307), kind=kOutput, calls=%fused_computation.21 | convolution fusion | flops 1212678144 | bytes 7474176 | tf_op jit(solution)/shard_map/dot_general | solution.py:543
  157.9 2.5 convolution_convert_fusion.1
  160.4 2.8 %fusion.87 = (bf16[768]{0:T(1024)(128)(2,1)S(1)}, bf16[1024,768]{1,0:T(8,128)(2,1)S(1)}) fusion(f32[1024,768]{1,0:T(8,128)S(1)} %get-tuple-element.117, f32[768]{0:T(1024)S(1)} %copy-done.30, bf16[1024,768]{1,0:T(8,128)(2,1)S(1)} %bitcast.299, bf16[768,768]{1,0:T(8,128)(2,1)S(1)} %bitcast.310), kind=kOutput, calls=%fused_computation.229 | convolution fusion | flops 1217395968 | bytes 7475712 | tf_op jit(solution)/shard_map/dot_general | solution.py:550
  165.7 3.2 %multiply_reduce_fusion = (bf16[768]{0:T(1024)(128)(2,1)S(1)}, bf16[768]{0:T(1024)(128)(2,1)S(1)}, bf16[768]{0:T(1024)(128)(2,1)S(1)}, bf16[768]{0:T(1024)(128)(...) fusion(f32[1024,768]{1,0:T(8,128)S(1)} %fusion.18, f32[1024]{0:T(1024)S(1)} %bitcast.324, ...), kind=kLoop, calls=%fused_computation.17 | loop fusion | flops 11793408 | bytes 15752192 | tf_op jit(solution)/shard_map/reduce_sum | solution.py:593
  172.6 2.8 %convolution_convert_fusion = bf16[768,768]{1,0:T(8,128)(2,1)S(1)} fusion(bf16[1024,768]{1,0:T(8,128)(2,1)S(1)} %copy-done.12, bf16[1024,768]{1,0:T(8,128)(2,1)} %copy-done.35), kind=kOutput, calls=%fused_computation.35 | convolution fusion | flops 1208549376 | bytes 4325376 | tf_op jit(solution)/shard_map/dot_general | solution.py:556
  175.6 4.4 %collective-permute-start.24 = (bf16[2,2,56,768]{3,2,1,0:T(8,128)(2,1)S(1)}, bf16[2,2,56,768]{3,2,1,0:T(8,128)(2,1)S(1)}, u32[]{:S(2)}, u32[]{:S(2)}) collective-permute-start(bf16[2,2,56,768]{3,2,1,0:T(8,128)(2,1)S(1)} %pad_maximum_fusion.4), channel_id=1, source_target_pairs={{0,4},{2,6},{4,0},{6,2},{8,12},{10,14},{12,8},{14,10},{16,20},{18,... | collective-permute-start | bytes 1032200 | tf_op jit(solution)/shard_map/ppermute | solution.py:237
  184.9 4.0 %collective-permute-done.24 = bf16[2,2,56,768]{3,2,1,0:T(8,128)(2,1)S(1)} collective-permute-done((bf16[2,2,56,768]{3,2,1,0:T(8,128)(2,1)S(1)}, bf16[2,2,56,768]{3,2,1,0:T(8,128)(2,1)S(1)}, u32[]{:S(2)}, u32[]{:S(2)}) %collective-permute-start.24) | collective-permute-done | bytes 344096 | tf_op jit(solution)/shard_map/ppermute | solution.py:237
  188.9 7.4 %collective-permute-done.23 = bf16[2,2,56,768]{3,2,1,0:T(8,128)(2,1)S(1)} collective-permute-done((bf16[2,2,56,768]{3,2,1,0:T(8,128)(2,1)S(1)}, bf16[2,2,56,768]{3,2,1,0:T(8,128)(2,1)S(1)}, u32[]{:S(2)}, u32[]{:S(2)}) %collective-permute-start.23) | collective-permute-done | bytes 344096 | tf_op jit(solution)/shard_map/ppermute | solution.py:237
  196.4 2.8 %collective-permute-start.27 = (bf16[2,56,768]{2,1,0:T(8,128)(2,1)S(1)}, bf16[2,56,768]{2,1,0:T(8,128)(2,1)S(1)}, u32[]{:S(2)}, u32[]{:S(2)}) collective-permute-start(bf16[2,56,768]{2,1,0:T(8,128)(2,1)S(1)} %get-tuple-element.79), channel_id=1, source_target_pairs={{0,24},{2,26},{4,28},{6,30},{8,0},{10,2},{12,4},{14,6},{16,8},{18,... | collective-permute-start | bytes 516104 | tf_op jit(solution)/shard_map/ppermute | solution.py:241
  200.7 7.6 %collective-permute-done.30 = bf16[4,96,768]{2,1,0:T(8,128)(2,1)S(1)} collective-permute-done((bf16[4,96,768]{2,1,0:T(8,128)(2,1)S(1)}, bf16[4,96,768]{2,1,0:T(8,128)(2,1)S(1)}, u32[]{:S(2)}, u32[]{:S(2)}) %collective-permute-start.30) | collective-permute-done | bytes 589856 | tf_op jit(solution)/shard_map/ppermute | solution.py:237
  208.4 3.9 %collective-permute-start.12 = (bf16[1,256,768]{2,1,0:T(8,128)(2,1)S(1)}, bf16[1,256,768]{2,1,0:T(8,128)(2,1)S(1)}, u32[]{:S(2)}, u32[]{:S(2)}) collective-permute-start(bf16[1,256,768]{2,1,0:T(8,128)(2,1)S(1)} %fusion.27), channel_id=1, source_target_pairs={{0,2},{2,0},{4,6},{6,4},{8,10},{10,8},{12,14},{14,12},{16,18},{18,... | collective-permute-start | bytes 1179656 | tf_op jit(solution)/shard_map/ppermute | solution.py:233
  215.2 3.5 %collective-permute-done.33 = bf16[96,768]{1,0:T(8,128)(2,1)S(1)} collective-permute-done((bf16[96,768]{1,0:T(8,128)(2,1)S(1)}, bf16[96,768]{1,0:T(8,128)(2,1)S(1)}, u32[]{:S(2)}, u32[]{:S(2)}) %collective-permute-start.33) | collective-permute-done | bytes 147488 | tf_op jit(solution)/shard_map/ppermute | solution.py:241
  218.6 3.7 %collective-permute-start.28 = (bf16[56,768]{1,0:T(8,128)(2,1)S(1)}, bf16[56,768]{1,0:T(8,128)(2,1)S(1)}, u32[]{:S(2)}, u32[]{:S(2)}) collective-permute-start(bf16[56,768]{1,0:T(8,128)(2,1)S(1)} %fusion.67), channel_id=1, source_target_pairs={{0,2},{2,0},{4,6},{6,4},{8,10},{10,8},{12,14},{14,12},{16,18},{18,... | collective-permute-start | bytes 258056 | tf_op jit(solution)/shard_map/ppermute | solution.py:233
  222.4 3.8 %collective-permute-done.32 = bf16[96,768]{1,0:T(8,128)(2,1)S(1)} collective-permute-done((bf16[96,768]{1,0:T(8,128)(2,1)S(1)}, bf16[96,768]{1,0:T(8,128)(2,1)S(1)}, u32[]{:S(2)}, u32[]{:S(2)}) %collective-permute-start.32) | collective-permute-done | bytes 147488 | tf_op jit(solution)/shard_map/ppermute | solution.py:241
  226.3 4.9 %collective-permute-done.28 = bf16[56,768]{1,0:T(8,128)(2,1)S(1)} collective-permute-done((bf16[56,768]{1,0:T(8,128)(2,1)S(1)}, bf16[56,768]{1,0:T(8,128)(2,1)S(1)}, u32[]{:S(2)}, u32[]{:S(2)}) %collective-permute-start.28) | collective-permute-done | bytes 86048 | tf_op jit(solution)/shard_map/ppermute | solution.py:233
  (277 shorter events, 80.4 us)
Async XLA Ops:
  7.2 139.8 %all-gather.3.cloned.1.call-start = ((), (), s32[]{:S(2)}) async-start(), calls=%async_computation | async-start | bytes 2654208 | tf_op jit(solution)/shard_map/all_gather | solution.py:276
  12.5 10.5 %collective-permute-start = (bf16[104,768]{1,0:T(8,128)(2,1)S(1)}, bf16[104,768]{1,0:T(8,128)(2,1)S(1)}, u32[]{:S(2)}, u32[]{:S(2)}) collective-permute-start(bf16[104,768]{1,0:T(8,128)(2,1)S(1)} %fusion.57), channel_id=1, source_target_pairs={{0,2},{2,0},{4,6},{6,4},{8,10},{10,8},{12,14},{14,12},{16,18},{18,... | collective-permute-start | bytes 479240 | tf_op jit(solution)/shard_map/ppermute | solution.py:233
  15.5 7.3 %collective-permute-start.3 = (bf16[24,768]{1,0:T(8,128)(2,1)S(1)}, bf16[24,768]{1,0:T(8,128)(2,1)S(1)}, u32[]{:S(2)}, u32[]{:S(2)}) collective-permute-start(bf16[24,768]{1,0:T(8,128)(2,1)S(1)} %dynamic-slice_convert_fusion.10), channel_id=1, source_target_pairs={{0,0},{1,4},{2,8},{3,12},{4,16},{5,20},{6,24},{7,28},{8,1},{9,5},{... | collective-permute-start | bytes 110600 | tf_op jit(solution)/shard_map/ppermute | solution.py:404
  16.3 28.3 %collective-permute-start.1 = (bf16[1,520,768]{2,1,0:T(8,128)(2,1)S(1)}, bf16[1,520,768]{2,1,0:T(8,128)(2,1)S(1)}, u32[]{:S(2)}, u32[]{:S(2)}) collective-permute-start(bf16[1,520,768]{2,1,0:T(8,128)(2,1)S(1)} %fusion.7), channel_id=1, source_target_pairs={{0,2},{2,0},{4,6},{6,4},{8,10},{10,8},{12,14},{14,12},{16,18},{18,... | collective-permute-start | bytes 2396168 | tf_op jit(solution)/shard_map/ppermute | solution.py:233
  24.6 11.1 %collective-permute-start.4 = (bf16[2,56,768]{2,1,0:T(8,128)(2,1)S(1)}, bf16[2,56,768]{2,1,0:T(8,128)(2,1)}, u32[]{:S(2)}, u32[]{:S(2)}) collective-permute-start(bf16[2,56,768]{2,1,0:T(8,128)(2,1)S(1)} %dynamic_update_slice.33), channel_id=1, source_target_pairs={{0,8},{2,10},{4,12},{6,14},{8,16},{10,18},{12,20},{14,22},{16,24},... | collective-permute-start | bytes 516104 | tf_op jit(solution)/shard_map/ppermute | solution.py:241
  25.7 15.2 %collective-permute-start.5 = (bf16[2,56,768]{2,1,0:T(8,128)(2,1)S(1)}, bf16[2,56,768]{2,1,0:T(8,128)(2,1)S(1)}, u32[]{:S(2)}, u32[]{:S(2)}) collective-permute-start(bf16[2,56,768]{2,1,0:T(8,128)(2,1)S(1)} %dynamic_update_slice.33), channel_id=1, source_target_pairs={{0,16},{2,18},{4,20},{6,22},{8,24},{10,26},{12,28},{14,30},{16,0},... | collective-permute-start | bytes 516104 | tf_op jit(solution)/shard_map/ppermute | solution.py:241
  30.9 12.7 %collective-permute-start.6 = (bf16[2,56,768]{2,1,0:T(8,128)(2,1)S(1)}, bf16[2,56,768]{2,1,0:T(8,128)(2,1)S(1)}, u32[]{:S(2)}, u32[]{:S(2)}) collective-permute-start(bf16[2,56,768]{2,1,0:T(8,128)(2,1)S(1)} %dynamic_update_slice.33), channel_id=1, source_target_pairs={{0,24},{2,26},{4,28},{6,30},{8,0},{10,2},{12,4},{14,6},{16,8},{18,... | collective-permute-start | bytes 516104 | tf_op jit(solution)/shard_map/ppermute | solution.py:241
  30.9 17.1 %collective-permute-start.7 = (bf16[2,56,768]{2,1,0:T(8,128)(2,1)S(1)}, bf16[2,56,768]{2,1,0:T(8,128)(2,1)}, u32[]{:S(2)}, u32[]{:S(2)}) collective-permute-start(bf16[2,56,768]{2,1,0:T(8,128)(2,1)S(1)} %dynamic_update_slice.33), channel_id=1, source_target_pairs={{0,4},{2,6},{4,0},{6,2},{8,12},{10,14},{12,8},{14,10},{16,20},{18,... | collective-permute-start | bytes 516104 | tf_op jit(solution)/shard_map/ppermute | solution.py:237
  35.7 13.3 %collective-permute-start.8 = (bf16[2,56,768]{2,1,0:T(8,128)(2,1)}, bf16[2,56,768]{2,1,0:T(8,128)(2,1)S(1)}, u32[]{:S(2)}, u32[]{:S(2)}) collective-permute-start(bf16[2,56,768]{2,1,0:T(8,128)(2,1)} %collective-permute-done.4), channel_id=1, source_target_pairs={{0,4},{2,6},{4,0},{6,2},{8,12},{10,14},{12,8},{14,10},{16,20},{18,... | collective-permute-start | bytes 516104 | tf_op jit(solution)/shard_map/ppermute | solution.py:237
  41.0 8.4 %collective-permute-start.9 = (bf16[2,56,768]{2,1,0:T(8,128)(2,1)S(1)}, bf16[2,56,768]{2,1,0:T(8,128)(2,1)S(1)}, u32[]{:S(2)}, u32[]{:S(2)}) collective-permute-start(bf16[2,56,768]{2,1,0:T(8,128)(2,1)S(1)} %collective-permute-done.5), channel_id=1, source_target_pairs={{0,4},{2,6},{4,0},{6,2},{8,12},{10,14},{12,8},{14,10},{16,20},{18,... | collective-permute-start | bytes 516104 | tf_op jit(solution)/shard_map/ppermute | solution.py:237
  43.6 8.7 %collective-permute-start.10 = (bf16[2,56,768]{2,1,0:T(8,128)(2,1)S(1)}, bf16[2,56,768]{2,1,0:T(8,128)(2,1)S(1)}, u32[]{:S(2)}, u32[]{:S(2)}) collective-permute-start(bf16[2,56,768]{2,1,0:T(8,128)(2,1)S(1)} %collective-permute-done.6), channel_id=1, source_target_pairs={{0,4},{2,6},{4,0},{6,2},{8,12},{10,14},{12,8},{14,10},{16,20},{18,... | collective-permute-start | bytes 516104 | tf_op jit(solution)/shard_map/ppermute | solution.py:237
  48.0 7.9 %collective-permute-start.2 = (bf16[2,1,520,768]{3,2,1,0:T(8,128)(2,1)S(1)}, bf16[2,1,520,768]{3,2,1,0:T(8,128)(2,1)}, u32[]{:S(2)}, u32[]{:S(2)}) collective-permute-start(bf16[2,1,520,768]{3,2,1,0:T(8,128)(2,1)S(1)} %get-tuple-element.78), channel_id=1, source_target_pairs={{0,1},{1,0},{2,3},{3,2},{4,5},{5,4},{6,7},{7,6},{8,9},{9,8},{10,11... | collective-permute-start | bytes 4792328 | tf_op jit(solution)/shard_map/ppermute | solution.py:252
  89.3 15.0 %collective-permute-start.13 = (bf16[4,96,768]{2,1,0:T(8,128)(2,1)}, bf16[4,96,768]{2,1,0:T(8,128)(2,1)}, u32[]{:S(2)}, u32[]{:S(2)}) collective-permute-start(bf16[4,96,768]{2,1,0:T(8,128)(2,1)} %fusion.23), channel_id=1, source_target_pairs={{0,4},{2,6},{4,0},{6,2},{8,12},{10,14},{12,8},{14,10},{16,20},{18,... | collective-permute-start | bytes 1769480 | tf_op jit(solution)/shard_map/ppermute | solution.py:237
  105.9 11.4 %collective-permute-start.18 = (bf16[96,768]{1,0:T(8,128)(2,1)S(1)}, bf16[96,768]{1,0:T(8,128)(2,1)S(1)}, u32[]{:S(2)}, u32[]{:S(2)}) collective-permute-start(bf16[96,768]{1,0:T(8,128)(2,1)S(1)} %get-tuple-element.88), channel_id=1, source_target_pairs={{0,24},{2,26},{4,28},{6,30},{8,0},{10,2},{12,4},{14,6},{16,8},{18,... | collective-permute-start | bytes 442376 | tf_op jit(solution)/shard_map/ppermute | solution.py:241
  110.3 17.6 %collective-permute-start.17 = (bf16[96,768]{1,0:T(8,128)(2,1)S(1)}, bf16[96,768]{1,0:T(8,128)(2,1)S(1)}, u32[]{:S(2)}, u32[]{:S(2)}) collective-permute-start(bf16[96,768]{1,0:T(8,128)(2,1)S(1)} %get-tuple-element.89), channel_id=1, source_target_pairs={{0,16},{2,18},{4,20},{6,22},{8,24},{10,26},{12,28},{14,30},{16,0},... | collective-permute-start | bytes 442376 | tf_op jit(solution)/shard_map/ppermute | solution.py:241
  115.1 12.8 %collective-permute-start.16 = (bf16[96,768]{1,0:T(8,128)(2,1)S(1)}, bf16[96,768]{1,0:T(8,128)(2,1)S(1)}, u32[]{:S(2)}, u32[]{:S(2)}) collective-permute-start(bf16[96,768]{1,0:T(8,128)(2,1)S(1)} %get-tuple-element.87), channel_id=1, source_target_pairs={{0,8},{2,10},{4,12},{6,14},{8,16},{10,18},{12,20},{14,22},{16,24},... | collective-permute-start | bytes 442376 | tf_op jit(solution)/shard_map/ppermute | solution.py:241
  128.7 5.2 %collective-permute-start.19 = (bf16[48,576]{1,0:T(8,128)(2,1)}, bf16[48,576]{1,0:T(8,128)(2,1)}, u32[]{:S(2)}, u32[]{:S(2)}) collective-permute-start(bf16[48,576]{1,0:T(8,128)(2,1)} %fusion.69), channel_id=1, source_target_pairs={{0,2},{2,0},{4,6},{6,4},{8,10},{10,8},{12,14},{14,12},{16,18},{18,... | collective-permute-start | bytes 165896 | tf_op jit(solution)/shard_map/ppermute | solution.py:233
  169.9 12.3 %collective-permute-start.11 = (bf16[2,1,256,768]{3,2,1,0:T(8,128)(2,1)}, bf16[2,1,256,768]{3,2,1,0:T(8,128)(2,1)}, u32[]{:S(2)}, u32[]{:S(2)}) collective-permute-start(bf16[2,1,256,768]{3,2,1,0:T(8,128)(2,1)} %bitcast.36), channel_id=1, source_target_pairs={{0,1},{1,0},{2,3},{3,2},{4,5},{5,4},{6,7},{7,6},{8,9},{9,8},{10,11... | collective-permute-start | bytes 2359304 | tf_op jit(solution)/shard_map/ppermute | solution.py:252
  170.4 13.1 %collective-permute-start.14 = (bf16[2,1,256,768]{3,2,1,0:T(8,128)(2,1)}, bf16[2,1,256,768]{3,2,1,0:T(8,128)(2,1)}, u32[]{:S(2)}, u32[]{:S(2)}) collective-permute-start(bf16[2,1,256,768]{3,2,1,0:T(8,128)(2,1)} %bitcast.50), channel_id=1, source_target_pairs={{0,1},{1,0},{2,3},{3,2},{4,5},{5,4},{6,7},{7,6},{8,9},{9,8},{10,11... | collective-permute-start | bytes 2359304 | tf_op jit(solution)/shard_map/ppermute | solution.py:252
  175.6 13.3 %collective-permute-start.24 = (bf16[2,2,56,768]{3,2,1,0:T(8,128)(2,1)S(1)}, bf16[2,2,56,768]{3,2,1,0:T(8,128)(2,1)S(1)}, u32[]{:S(2)}, u32[]{:S(2)}) collective-permute-start(bf16[2,2,56,768]{3,2,1,0:T(8,128)(2,1)S(1)} %pad_maximum_fusion.4), channel_id=1, source_target_pairs={{0,4},{2,6},{4,0},{6,2},{8,12},{10,14},{12,8},{14,10},{16,20},{18,... | collective-permute-start | bytes 1032200 | tf_op jit(solution)/shard_map/ppermute | solution.py:237
  180.0 16.3 %collective-permute-start.23 = (bf16[2,2,56,768]{3,2,1,0:T(8,128)(2,1)S(1)}, bf16[2,2,56,768]{3,2,1,0:T(8,128)(2,1)S(1)}, u32[]{:S(2)}, u32[]{:S(2)}) collective-permute-start(bf16[2,2,56,768]{3,2,1,0:T(8,128)(2,1)S(1)} %pad_maximum_fusion.3), channel_id=1, source_target_pairs={{0,4},{2,6},{4,0},{6,2},{8,12},{10,14},{12,8},{14,10},{16,20},{18,... | collective-permute-start | bytes 1032200 | tf_op jit(solution)/shard_map/ppermute | solution.py:237
  180.2 28.1 %collective-permute-start.30 = (bf16[4,96,768]{2,1,0:T(8,128)(2,1)S(1)}, bf16[4,96,768]{2,1,0:T(8,128)(2,1)S(1)}, u32[]{:S(2)}, u32[]{:S(2)}) collective-permute-start(bf16[4,96,768]{2,1,0:T(8,128)(2,1)S(1)} %dynamic-slice_bitcast_fusion), channel_id=1, source_target_pairs={{0,4},{2,6},{4,0},{6,2},{8,12},{10,14},{12,8},{14,10},{16,20},{18,... | collective-permute-start | bytes 1769480 | tf_op jit(solution)/shard_map/ppermute | solution.py:237
  196.4 16.0 %collective-permute-start.27 = (bf16[2,56,768]{2,1,0:T(8,128)(2,1)S(1)}, bf16[2,56,768]{2,1,0:T(8,128)(2,1)S(1)}, u32[]{:S(2)}, u32[]{:S(2)}) collective-permute-start(bf16[2,56,768]{2,1,0:T(8,128)(2,1)S(1)} %get-tuple-element.79), channel_id=1, source_target_pairs={{0,24},{2,26},{4,28},{6,30},{8,0},{10,2},{12,4},{14,6},{16,8},{18,... | collective-permute-start | bytes 516104 | tf_op jit(solution)/shard_map/ppermute | solution.py:241
  199.2 15.7 %collective-permute-start.26 = (bf16[2,56,768]{2,1,0:T(8,128)(2,1)S(1)}, bf16[2,56,768]{2,1,0:T(8,128)(2,1)S(1)}, u32[]{:S(2)}, u32[]{:S(2)}) collective-permute-start(bf16[2,56,768]{2,1,0:T(8,128)(2,1)S(1)} %get-tuple-element.76), channel_id=1, source_target_pairs={{0,16},{2,18},{4,20},{6,22},{8,24},{10,26},{12,28},{14,30},{16,0},... | collective-permute-start | bytes 516104 | tf_op jit(solution)/shard_map/ppermute | solution.py:241
  199.2 15.7 %collective-permute-start.25 = (bf16[2,56,768]{2,1,0:T(8,128)(2,1)S(1)}, bf16[2,56,768]{2,1,0:T(8,128)(2,1)S(1)}, u32[]{:S(2)}, u32[]{:S(2)}) collective-permute-start(bf16[2,56,768]{2,1,0:T(8,128)(2,1)S(1)} %get-tuple-element.75), channel_id=1, source_target_pairs={{0,8},{2,10},{4,12},{6,14},{8,16},{10,18},{12,20},{14,22},{16,24},... | collective-permute-start | bytes 516104 | tf_op jit(solution)/shard_map/ppermute | solution.py:241
  208.4 27.2 %collective-permute-start.12 = (bf16[1,256,768]{2,1,0:T(8,128)(2,1)S(1)}, bf16[1,256,768]{2,1,0:T(8,128)(2,1)S(1)}, u32[]{:S(2)}, u32[]{:S(2)}) collective-permute-start(bf16[1,256,768]{2,1,0:T(8,128)(2,1)S(1)} %fusion.27), channel_id=1, source_target_pairs={{0,2},{2,0},{4,6},{6,4},{8,10},{10,8},{12,14},{14,12},{16,18},{18,... | collective-permute-start | bytes 1179656 | tf_op jit(solution)/shard_map/ppermute | solution.py:233
  212.3 20.8 %collective-permute-start.15 = (bf16[1,256,768]{2,1,0:T(8,128)(2,1)S(1)}, bf16[1,256,768]{2,1,0:T(8,128)(2,1)S(1)}, u32[]{:S(2)}, u32[]{:S(2)}) collective-permute-start(bf16[1,256,768]{2,1,0:T(8,128)(2,1)S(1)} %fusion.28), channel_id=1, source_target_pairs={{0,2},{2,0},{4,6},{6,4},{8,10},{10,8},{12,14},{14,12},{16,18},{18,... | collective-permute-start | bytes 1179656 | tf_op jit(solution)/shard_map/ppermute | solution.py:233
  212.4 6.2 %collective-permute-start.33 = (bf16[96,768]{1,0:T(8,128)(2,1)S(1)}, bf16[96,768]{1,0:T(8,128)(2,1)S(1)}, u32[]{:S(2)}, u32[]{:S(2)}) collective-permute-start(bf16[96,768]{1,0:T(8,128)(2,1)S(1)} %get-tuple-element.85), channel_id=1, source_target_pairs={{0,24},{2,26},{4,28},{6,30},{8,0},{10,2},{12,4},{14,6},{16,8},{18,... | collective-permute-start | bytes 442376 | tf_op jit(solution)/shard_map/ppermute | solution.py:241
  214.9 11.2 %collective-permute-start.32 = (bf16[96,768]{1,0:T(8,128)(2,1)S(1)}, bf16[96,768]{1,0:T(8,128)(2,1)S(1)}, u32[]{:S(2)}, u32[]{:S(2)}) collective-permute-start(bf16[96,768]{1,0:T(8,128)(2,1)S(1)} %get-tuple-element.86), channel_id=1, source_target_pairs={{0,16},{2,18},{4,20},{6,22},{8,24},{10,26},{12,28},{14,30},{16,0},... | collective-permute-start | bytes 442376 | tf_op jit(solution)/shard_map/ppermute | solution.py:241
  214.9 11.2 %collective-permute-start.31 = (bf16[96,768]{1,0:T(8,128)(2,1)S(1)}, bf16[96,768]{1,0:T(8,128)(2,1)S(1)}, u32[]{:S(2)}, u32[]{:S(2)}) collective-permute-start(bf16[96,768]{1,0:T(8,128)(2,1)S(1)} %get-tuple-element.84), channel_id=1, source_target_pairs={{0,8},{2,10},{4,12},{6,14},{8,16},{10,18},{12,20},{14,22},{16,24},... | collective-permute-start | bytes 442376 | tf_op jit(solution)/shard_map/ppermute | solution.py:241
  218.6 12.6 %collective-permute-start.28 = (bf16[56,768]{1,0:T(8,128)(2,1)S(1)}, bf16[56,768]{1,0:T(8,128)(2,1)S(1)}, u32[]{:S(2)}, u32[]{:S(2)}) collective-permute-start(bf16[56,768]{1,0:T(8,128)(2,1)S(1)} %fusion.67), channel_id=1, source_target_pairs={{0,2},{2,0},{4,6},{6,4},{8,10},{10,8},{12,14},{14,12},{16,18},{18,... | collective-permute-start | bytes 258056 | tf_op jit(solution)/shard_map/ppermute | solution.py:233
  231.3 5.2 %collective-permute-start.29 = (bf16[2,56,768]{2,1,0:T(8,128)(2,1)S(1)}, bf16[2,56,768]{2,1,0:T(8,128)(2,1)S(1)}, u32[]{:S(2)}, u32[]{:S(2)}) collective-permute-start(bf16[2,56,768]{2,1,0:T(8,128)(2,1)S(1)} %pad_maximum_fusion.10), channel_id=1, source_target_pairs={{0,1},{1,0},{2,3},{3,2},{4,5},{5,4},{6,7},{7,6},{8,9},{9,8},{10,11... | collective-permute-start | bytes 516104 | tf_op jit(solution)/shard_map/ppermute | solution.py:252
  (41 other events, 168.9 us)
Sparse Core Ops, SparseCore 0:
  32.9 51.2 all-gather.2
where the time goes:
time: 248 us
  waiting for transfers between devices  65.7 us (26%)
  starting transfers between devices  52.7 us (21%)
  local copies, waits for them, and re-layouts  40 us (16%)
  other arithmetic  36.4 us (15%)
  Pallas kernels  22.4 us (9%)
  between operations  15.4 us (6%)
  matrix products  14.9 us (6%)
    ppermute x8, waiting for transfers between devices, from_pair(): lax.ppermute(array, 'shard', [(s, s ^ step) for s in range(self.shards)])  34 us
    ppermute x12, waiting for transfers between devices, along_line(): lax.ppermute(array, 'shard', [(s, (s // block + hops) % self.lines * bloc...  26.7 us
    pallas_call x1, Pallas kernels, attention(): pl.pallas_call(functools.partial(attention_kernel, ways, heads), grid=(se...  22.4 us
    ppermute x12, starting transfers between devices, along_line(): lax.ppermute(array, 'shard', [(s, (s // block + hops) % self.lines * bloc...  20.4 us
    ppermute x6, starting transfers between devices, from_twin(): lax.ppermute(array, 'shard', [(s, s ^ 1) for s in range(self.shards)])  15.1 us
    ppermute x8, starting transfers between devices, from_pair(): lax.ppermute(array, 'shard', [(s, s ^ step) for s in range(self.shards)])  13.1 us
    convert_element_type x6, local copies, waits for them, and re-layouts, step(): totals = (first_total.reshape(ways, rows, 3, out_cols).transpose(1, 2, 0,...  8.41 us
    sub x5, other arithmetic, adamw(): weight - learn_rate * (first_hat / (jnp.sqrt(second_hat) + adam_eps) + de...  8.25 us
  transfers between devices with their start and end apart: 36, of which 14 were waited for; matrix products, arithmetic and copies ran while one was open for 23% of the time, Pallas kernels for 9%

commit v1 on v0

--- a/solution.py
+++ b/solution.py
@@ -311,7 +311,8 @@
 
         order = [hops for hops in range(1, self.lines)] + [0]
         if pieces == 1:
-            merged = keep.astype(wide) + self.from_pair(give).astype(wide)
+            far = self.from_pair(give)
+            merged = keep.astype(wide) + far.astype(wide)
             if before:
                 merged = after(merged, *before)
             if marks is not None:
@@ -322,14 +323,20 @@
             size = -(-self.lines // pieces)
             for start in range(0, self.lines, size):
                 chosen = order[start : start + size]
-                far = self.from_pair(jnp.stack([block(give, hops) for hops in chosen]))
+                far = jnp.stack([block(give, hops) for hops in chosen])
+                far = self.from_pair(far)
                 if before:
                     far = after(far, *before)
+                if marks is not None:
+                    marks.append(far)
                 for place, hops in enumerate(chosen):
-                    sums[hops] = block(keep, hops).astype(wide) + far[place].astype(wide)
+                    term = block(keep, hops).astype(wide) + far[place].astype(wide)
+                    sums[hops] = term.astype(jnp.bfloat16) if hops else term
         total = sums[0]
         for hops in range(1, self.lines):
-            total = total + self.along_line(sums[hops].astype(jnp.bfloat16), hops).astype(wide)
+            give = sums[hops].astype(jnp.bfloat16)
+            far = self.along_line(give, hops)
+            total = total + far.astype(wide)
         return total
 
     def gather_sequences(self, array):
@@ -349,13 +356,15 @@
         slots = partial.reshape((self.replicas, self.twins, batch) + shape[1:])
         total = slots[0]
         for hops in range(1, self.replicas):
-            total = total + self.to_replica(slots[hops].astype(wire), hops).astype(wide)
+            far = self.to_replica(slots[hops].astype(wire), hops)
+            total = total + far.astype(wide)
         own = total[0]
         if self.twins == 2:
             give = total[1].astype(wire)
             if marks is not None:
                 marks.append(give)
-            own = own + self.from_twin(give).astype(wide)
+            far = self.from_twin(give)
+            own = own + far.astype(wide)
         return own
 
 
@@ -535,11 +544,6 @@
     )
     marks = []
     first_sum = group.scatter(first_grad, 1, marks)
-    first_total = group.unshare(first_sum[:, : 3 * out_cols].reshape(twins, rows, -1))
-    out_sum = first_sum[:, 3 * out_cols :].astype(half).reshape(ways, out_rows, out_cols)
-    out_sum = out_sum.transpose(1, 0, 2).reshape(out_rows, D)
-    out_total = group.from_replicas(group.to_holders(out_sum)).reshape(rows, D)
-
     hidden = jnp.dot(normed_mlp, in_all, preferred_element_type=wide) + bias_in_own
     share_below = 0.5 + 0.5 * lax.erf(hidden * 0.5**0.5)
     act_half = (hidden * share_below).astype(half)
@@ -547,9 +551,8 @@
         act_half, cot_flat, (((0,), (0,)), ((), ())), preferred_element_type=wide
     ).astype(half)
     sent = []
-    grad_act = lax.dot_general(
-        after(cot_flat, grad_down, *marks), down_all, (((1,), (1,)), ((), ())), preferred_element_type=wide
-    )
+    back_cot = after(cot_flat, grad_down, *marks)
+    grad_act = contract(back_cot, down_all, 1, 1)
     density = jnp.exp(-0.5 * hidden * hidden) * (2.0 * np.pi) ** -0.5
     grad_hidden = grad_act * (share_below + hidden * density)
     hidden_half = grad_hidden.astype(half)
@@ -567,9 +570,11 @@
     own = batch * length
     own_unit = unit[:own]
     own_cot = cotangent.reshape(own, D).astype(wide)
-    slope = group.reduce_sequences(partial_slope.reshape(seqs, length, D), sent).reshape(own, D)
+    slope = group.reduce_sequences(partial_slope.reshape(seqs, length, D), sent)
+    slope = slope.reshape(own, D)
+    down_marks = []
     down_total = group.from_replicas(
-        group.scatter(grad_down.reshape(groups, units, D), before=sent[:1]).astype(half)
+        group.scatter(grad_down.reshape(groups, units, D), 1, down_marks).astype(half)
     )
     scale = lax.rsqrt(spread[:own] + norm_eps)
     back = scale * (
@@ -602,7 +607,13 @@
         vector_grad.astype(half), ((0, 0), (0, 0), (0, vec_rows * width - vec_size))
     ).reshape(groups, twins, vec_rows, width)
     in_grad = jnp.concatenate([grad_in.reshape(groups, twins, rows, width), vector_grad], axis=2)
-    in_total = group.unshare(group.scatter(in_grad, 2, before=sent))
+    in_marks = []
+    in_total = group.unshare(group.scatter(in_grad, 2, in_marks, sent))
+    first_sum = after(first_sum, *in_marks)
+    first_total = group.unshare(first_sum[:, : 3 * out_cols].reshape(twins, rows, -1))
+    out_sum = first_sum[:, 3 * out_cols :].astype(half).reshape(ways, out_rows, out_cols)
+    out_sum = out_sum.transpose(1, 0, 2).reshape(out_rows, D)
+    out_total = group.from_replicas(group.to_holders(out_sum)).reshape(rows, D)
     vec_total = jnp.sum(in_total[:, rows:].astype(wide), axis=0).reshape(-1)[:vec_size]
 
     totals = (

time: 248 us -> 247 us (level)
  starting transfers between devices: 52.7 us -> 47.5 us
  other arithmetic: 36.4 us -> 40 us
  local copies, waits for them, and re-layouts: 40 us -> 43.2 us
  waiting for transfers between devices: 65.7 us -> 62.8 us
    ppermute x8, waiting for transfers between devices: 34 us -> 27.1 us  [from_pair(): lax.ppermute(array, 'shard', [(s, s ^ step) for s in range(self.shards)])]
    ppermute x12, starting transfers between devices: 20.4 us -> 26.8 us  [along_line(): lax.ppermute(array, 'shard', [(s, (s // block + hops) % self.lines * bloc...]
    ppermute x8, starting transfers between devices: 13.1 us -> 7.38 us  [from_pair(): lax.ppermute(array, 'shard', [(s, s ^ step) for s in range(self.shards)])]
    ppermute x6, starting transfers between devices: 15.1 us -> 11.3 us  [from_twin(): lax.ppermute(array, 'shard', [(s, s ^ 1) for s in range(self.shards)])]
    ppermute x12, waiting for transfers between devices: 26.7 us -> 29.7 us  [along_line(): lax.ppermute(array, 'shard', [(s, (s // block + hops) % self.lines * bloc...]
    unnamed x82 -> x114, local copies, waits for them, and re-layouts: 7.95 us -> 8.69 us
  transfers between devices with their start and end apart: 36 -> 36, of which waited for: 14 -> 15; matrix products, arithmetic and copies ran while one was open for 23% -> 25% of each run, Pallas kernels for 9% -> 9%
where the time goes in v1:
time: 247 us; the launch traced here: 246 us
  waiting for transfers between devices  62.8 us (25%)
  starting transfers between devices  47.5 us (19%)
  local copies, waits for them, and re-layouts  43.2 us (17%)
  other arithmetic  40 us (16%)
  Pallas kernels  22.4 us (9%)
  between operations  15.4 us (6%)
  matrix products  15 us (6%)
    ppermute x12, waiting for transfers between devices, along_line(): lax.ppermute(array, 'shard', [(s, (s // block + hops) % self.lines * bloc...  29.7 us
    ppermute x8, waiting for transfers between devices, from_pair(): lax.ppermute(array, 'shard', [(s, s ^ step) for s in range(self.shards)])  27.1 us
    ppermute x12, starting transfers between devices, along_line(): lax.ppermute(array, 'shard', [(s, (s // block + hops) % self.lines * bloc...  26.8 us
    pallas_call x1, Pallas kernels, attention(): pl.pallas_call(functools.partial(attention_kernel, ways, heads), grid=(se...  22.4 us
    ppermute x6, starting transfers between devices, from_twin(): lax.ppermute(array, 'shard', [(s, s ^ 1) for s in range(self.shards)])  11.3 us
    unnamed x114, local copies, waits for them, and re-layouts  8.69 us
    convert_element_type x6, local copies, waits for them, and re-layouts, step(): totals = (first_total.reshape(ways, rows, 3, out_cols).transpose(1, 2, 0,...  8.41 us
    ppermute x8, starting transfers between devices, from_pair(): lax.ppermute(array, 'shard', [(s, s ^ step) for s in range(self.shards)])  7.38 us
  transfers between devices with their start and end apart: 36, of which 15 were waited for; matrix products, arithmetic and copies ran while one was open for 25% of the time, Pallas kernels for 9%

profile of v1, /device:TPU:0, one launch (start us, length us, event | category | flops | bytes accessed | tf_op | source)
XLA Modules:
  0.0 246.2 jit_solution(18292043907367428872)
XLA Ops:
  12.5 3.0 %collective-permute-start = (bf16[104,768]{1,0:T(8,128)(2,1)S(1)}, bf16[104,768]{1,0:T(8,128)(2,1)S(1)}, u32[]{:S(2)}, u32[]{:S(2)}) collective-permute-start(bf16[104,768]{1,0:T(8,128)(2,1)S(1)} %fusion.57), channel_id=1, source_target_pairs={{0,2},{2,0},{4,6},{6,4},{8,10},{10,8},{12,14},{14,12},{16,18},{18,... | collective-permute-start | bytes 479240 | tf_op jit(solution)/shard_map/ppermute | solution.py:233
  17.2 4.3 %collective-permute-start.1 = (bf16[1,520,768]{2,1,0:T(8,128)(2,1)S(1)}, bf16[1,520,768]{2,1,0:T(8,128)(2,1)S(1)}, u32[]{:S(2)}, u32[]{:S(2)}) collective-permute-start(bf16[1,520,768]{2,1,0:T(8,128)(2,1)S(1)} %fusion.7), channel_id=1, source_target_pairs={{0,2},{2,0},{4,6},{6,4},{8,10},{10,8},{12,14},{14,12},{16,18},{18,... | collective-permute-start | bytes 2396168 | tf_op jit(solution)/shard_map/ppermute | solution.py:233
  26.6 5.2 %collective-permute-start.5 = (bf16[2,56,768]{2,1,0:T(8,128)(2,1)S(1)}, bf16[2,56,768]{2,1,0:T(8,128)(2,1)S(1)}, u32[]{:S(2)}, u32[]{:S(2)}) collective-permute-start(bf16[2,56,768]{2,1,0:T(8,128)(2,1)S(1)} %dynamic_update_slice.33), channel_id=1, source_target_pairs={{0,16},{2,18},{4,20},{6,22},{8,24},{10,26},{12,28},{14,30},{16,0},... | collective-permute-start | bytes 516104 | tf_op jit(solution)/shard_map/ppermute | solution.py:241
  33.7 2.7 %collective-permute-done.4 = bf16[2,56,768]{2,1,0:T(8,128)(2,1)S(1)} collective-permute-done((bf16[2,56,768]{2,1,0:T(8,128)(2,1)S(1)}, bf16[2,56,768]{2,1,0:T(8,128)(2,1)S(1)}, u32[]{:S(2)}, u32[]{:S(2)}) %collective-permute-start.4) | collective-permute-done | bytes 172064 | tf_op jit(solution)/shard_map/ppermute | solution.py:241
  38.1 3.7 %collective-permute-done.5 = bf16[2,56,768]{2,1,0:T(8,128)(2,1)S(1)} collective-permute-done((bf16[2,56,768]{2,1,0:T(8,128)(2,1)S(1)}, bf16[2,56,768]{2,1,0:T(8,128)(2,1)S(1)}, u32[]{:S(2)}, u32[]{:S(2)}) %collective-permute-start.5) | collective-permute-done | bytes 172064 | tf_op jit(solution)/shard_map/ppermute | solution.py:241
  41.8 2.6 %collective-permute-start.9 = (bf16[2,56,768]{2,1,0:T(8,128)(2,1)S(1)}, bf16[2,56,768]{2,1,0:T(8,128)(2,1)S(1)}, u32[]{:S(2)}, u32[]{:S(2)}) collective-permute-start(bf16[2,56,768]{2,1,0:T(8,128)(2,1)S(1)} %collective-permute-done.5), channel_id=1, source_target_pairs={{0,4},{2,6},{4,0},{6,2},{8,12},{10,14},{12,8},{14,10},{16,20},{18,... | collective-permute-start | bytes 516104 | tf_op jit(solution)/shard_map/ppermute | solution.py:237
  45.4 2.6 %fusion.79 = (bf16[1,2,1,520,768]{4,3,1,2,0:T(8,128)(2,1)}, bf16[2,1,520,768]{3,2,1,0:T(8,128)(2,1)S(1)}) fusion(bf16[1,1,520,768]{3,2,1,0:T(8,128)(2,1)} %bitcast.311, bf16[1,1,520,768]{3,2,1,0:T(8,128)(2,1)S(1)} %bitcast.293), kind=kLoop, calls=%fused_computation.226 | loop fusion | flops 798720 | bytes 4792320 | tf_op jit(solution)/shard_map/stack | solution.py:349
  50.2 2.9 %collective-permute-done.10 = bf16[2,56,768]{2,1,0:T(8,128)(2,1)S(1)} collective-permute-done((bf16[2,56,768]{2,1,0:T(8,128)(2,1)S(1)}, bf16[2,56,768]{2,1,0:T(8,128)(2,1)S(1)}, u32[]{:S(2)}, u32[]{:S(2)}) %collective-permute-start.10) | collective-permute-done | bytes 172064 | tf_op jit(solution)/shard_map/ppermute | solution.py:237
  56.7 2.2 pad_maximum_fusion
  64.5 22.4 %attention_block.1 = (bf16[1024,192]{1,0:T(8,128)(2,1)}, f32[1024,768]{1,0:T(8,128)}, f32[1024,768]{1,0:T(8,128)}, f32[4,1,768]{2,1,0:T(1,128)}, bf16[768,768]{1,0:T(8,128)(2,1)}, /*index=5*/bf16[4,192,192]{2,1,0:T(8,128)(2,1)}) custom-call(bf16[1024,768]{1,0:T(8,128)(2,1)} %add_convert_fusion.2.normed_ref, bf16[1024,768]{1,0:T(8,128)(2,1)} %bitcast.297, ...), custom_call_target="tpu_custom_call" | custom-call | flops 6442450944 | bytes 18874368 | tf_op jit(solution)/shard_map/attention_block/pallas_call | solution.py:160
  95.1 10.1 %collective-permute-done.13 = bf16[4,96,768]{2,1,0:T(8,128)(2,1)} collective-permute-done((bf16[4,96,768]{2,1,0:T(8,128)(2,1)}, bf16[4,96,768]{2,1,0:T(8,128)(2,1)}, u32[]{:S(2)}, u32[]{:S(2)}) %collective-permute-start.13) | collective-permute-done | bytes 589856 | tf_op jit(solution)/shard_map/ppermute | solution.py:237
  106.6 3.5 %collective-permute-start.18 = (bf16[96,768]{1,0:T(8,128)(2,1)S(1)}, bf16[96,768]{1,0:T(8,128)(2,1)S(1)}, u32[]{:S(2)}, u32[]{:S(2)}) collective-permute-start(bf16[96,768]{1,0:T(8,128)(2,1)S(1)} %get-tuple-element.88), channel_id=1, source_target_pairs={{0,24},{2,26},{4,28},{6,30},{8,0},{10,2},{12,4},{14,6},{16,8},{18,... | collective-permute-start | bytes 442376 | tf_op jit(solution)/shard_map/ppermute | solution.py:241
  110.1 4.8 %collective-permute-start.17 = (bf16[96,768]{1,0:T(8,128)(2,1)S(1)}, bf16[96,768]{1,0:T(8,128)(2,1)S(1)}, u32[]{:S(2)}, u32[]{:S(2)}) collective-permute-start(bf16[96,768]{1,0:T(8,128)(2,1)S(1)} %get-tuple-element.89), channel_id=1, source_target_pairs={{0,16},{2,18},{4,20},{6,22},{8,24},{10,26},{12,28},{14,30},{16,0},... | collective-permute-start | bytes 442376 | tf_op jit(solution)/shard_map/ppermute | solution.py:241
  117.1 10.7 %collective-permute-done.17 = bf16[96,768]{1,0:T(8,128)(2,1)S(1)} collective-permute-done((bf16[96,768]{1,0:T(8,128)(2,1)S(1)}, bf16[96,768]{1,0:T(8,128)(2,1)S(1)}, u32[]{:S(2)}, u32[]{:S(2)}) %collective-permute-start.17) | collective-permute-done | bytes 147488 | tf_op jit(solution)/shard_map/ppermute | solution.py:241
  130.0 4.0 %multiply_convert_fusion = (bf16[1024,768]{1,0:T(8,128)(2,1)S(1)}, f32[1024,768]{1,0:T(8,128)S(1)}) fusion(f32[768]{0:T(1024)S(1)} %copy-done.46, bf16[1024,768]{1,0:T(8,128)(2,1)S(1)} %bitcast.300, bf16[768,768]{1,0:T(8,128)(2,1)S(1)} %bitcast.307), kind=kOutput, calls=%fused_computation.21 | convolution fusion | flops 1212678144 | bytes 7474176 | tf_op jit(solution)/shard_map/dot_general | solution.py:547
  138.7 2.5 %convolution_convert_fusion.1 = bf16[768,768]{1,0:T(8,128)(2,1)} fusion(bf16[1024,768]{1,0:T(8,128)(2,1)S(1)} %get-tuple-element.116, bf16[1024,768]{1,0:T(8,128)(2,1)S(1)} %bitcast.298), kind=kOutput, calls=%fused_computation.36 | convolution fusion | flops 1208549376 | bytes 4325376 | tf_op jit(solution)/shard_map/dot_general | solution.py:550
  141.3 2.8 %fusion.87 = (bf16[768]{0:T(1024)(128)(2,1)S(1)}, bf16[1024,768]{1,0:T(8,128)(2,1)S(1)}) fusion(f32[1024,768]{1,0:T(8,128)S(1)} %get-tuple-element.117, f32[768]{0:T(1024)S(1)} %copy-done.46, bf16[1024,768]{1,0:T(8,128)(2,1)S(1)} %bitcast.299, bf16[768,768]{1,0:T(8,128)(2,1)S(1)} %bitcast.310), kind=kOutput, calls=%fused_computation.229 | convolution fusion | flops 1217395968 | bytes 7475712 | tf_op jit(solution)/shard_map/dot_general | solution.py:50
  146.6 3.2 %multiply_reduce_fusion = (bf16[768]{0:T(1024)(128)(2,1)S(1)}, bf16[768]{0:T(1024)(128)(2,1)S(1)}, bf16[768]{0:T(1024)(128)(2,1)S(1)}, bf16[768]{0:T(1024)(128)(...) fusion(f32[1024,768]{1,0:T(8,128)S(1)} %fusion.18, f32[1024]{0:T(1024)S(1)} %bitcast.324, ...), kind=kLoop, calls=%fused_computation.17 | loop fusion | flops 11793408 | bytes 15752192 | tf_op jit(solution)/shard_map/reduce_sum | solution.py:598
  155.3 2.8 %convolution_convert_fusion = bf16[768,768]{1,0:T(8,128)(2,1)S(1)} fusion(bf16[1024,768]{1,0:T(8,128)(2,1)S(1)} %copy-done.19, bf16[1024,768]{1,0:T(8,128)(2,1)} %copy-done.51), kind=kOutput, calls=%fused_computation.35 | convolution fusion | flops 1208549376 | bytes 4325376 | tf_op jit(solution)/shard_map/dot_general | solution.py:559
  158.2 11.0 %collective-permute-done.30 = bf16[4,96,768]{2,1,0:T(8,128)(2,1)} collective-permute-done((bf16[4,96,768]{2,1,0:T(8,128)(2,1)}, bf16[4,96,768]{2,1,0:T(8,128)(2,1)}, u32[]{:S(2)}, u32[]{:S(2)}) %collective-permute-start.30) | collective-permute-done | bytes 589856 | tf_op jit(solution)/shard_map/ppermute | solution.py:237
  170.6 1.9 collective-permute-start.31
  172.6 4.2 %collective-permute-done.33 = bf16[96,768]{1,0:T(8,128)(2,1)S(1)} collective-permute-done((bf16[96,768]{1,0:T(8,128)(2,1)S(1)}, bf16[96,768]{1,0:T(8,128)(2,1)S(1)}, u32[]{:S(2)}, u32[]{:S(2)}) %collective-permute-start.33) | collective-permute-done | bytes 147488 | tf_op jit(solution)/shard_map/ppermute | solution.py:241
  177.6 5.5 %collective-permute-done.32 = bf16[96,768]{1,0:T(8,128)(2,1)S(1)} collective-permute-done((bf16[96,768]{1,0:T(8,128)(2,1)S(1)}, bf16[96,768]{1,0:T(8,128)(2,1)S(1)}, u32[]{:S(2)}, u32[]{:S(2)}) %collective-permute-start.32) | collective-permute-done | bytes 147488 | tf_op jit(solution)/shard_map/ppermute | solution.py:241
  188.6 2.0 collective-permute-start.15
  194.9 1.9 fusion.31
  196.9 7.0 %collective-permute-start.27 = (bf16[2,56,768]{2,1,0:T(8,128)(2,1)}, bf16[2,56,768]{2,1,0:T(8,128)(2,1)}, u32[]{:S(2)}, u32[]{:S(2)}) collective-permute-start(bf16[2,56,768]{2,1,0:T(8,128)(2,1)} %get-tuple-element.79), channel_id=1, source_target_pairs={{0,24},{2,26},{4,28},{6,30},{8,0},{10,2},{12,4},{14,6},{16,8},{18,... | collective-permute-start | bytes 516104 | tf_op jit(solution)/shard_map/ppermute | solution.py:241
  203.9 4.2 %collective-permute-done.21 = bf16[48,576]{1,0:T(8,128)(2,1)} collective-permute-done((bf16[48,576]{1,0:T(8,128)(2,1)}, bf16[48,576]{1,0:T(8,128)(2,1)}, u32[]{:S(2)}, u32[]{:S(2)}) %collective-permute-start.21) | collective-permute-done | bytes 55328 | tf_op jit(solution)/shard_map/ppermute | solution.py:233
  209.3 3.0 %collective-permute-start.26 = (bf16[2,56,768]{2,1,0:T(8,128)(2,1)}, bf16[2,56,768]{2,1,0:T(8,128)(2,1)S(1)}, u32[]{:S(2)}, u32[]{:S(2)}) collective-permute-start(bf16[2,56,768]{2,1,0:T(8,128)(2,1)} %get-tuple-element.76), channel_id=1, source_target_pairs={{0,16},{2,18},{4,20},{6,22},{8,24},{10,26},{12,28},{14,30},{16,0},... | collective-permute-start | bytes 516104 | tf_op jit(solution)/shard_map/ppermute | solution.py:241
  216.7 2.2 reshape.463
  219.0 2.3 copy.82
  221.3 2.2 reshape.450
  233.4 1.9 fusion.12
  (309 shorter events, 85.3 us)
Async XLA Ops:
  7.2 120.6 %all-gather.3.cloned.1.call-start = ((), (), s32[]{:S(2)}) async-start(), calls=%async_computation | async-start | bytes 2654208 | tf_op jit(solution)/shard_map/all_gather | solution.py:276
  12.5 11.4 %collective-permute-start = (bf16[104,768]{1,0:T(8,128)(2,1)S(1)}, bf16[104,768]{1,0:T(8,128)(2,1)S(1)}, u32[]{:S(2)}, u32[]{:S(2)}) collective-permute-start(bf16[104,768]{1,0:T(8,128)(2,1)S(1)} %fusion.57), channel_id=1, source_target_pairs={{0,2},{2,0},{4,6},{6,4},{8,10},{10,8},{12,14},{14,12},{16,18},{18,... | collective-permute-start | bytes 479240 | tf_op jit(solution)/shard_map/ppermute | solution.py:233
  16.4 7.3 %collective-permute-start.3 = (bf16[24,768]{1,0:T(8,128)(2,1)S(1)}, bf16[24,768]{1,0:T(8,128)(2,1)S(1)}, u32[]{:S(2)}, u32[]{:S(2)}) collective-permute-start(bf16[24,768]{1,0:T(8,128)(2,1)S(1)} %dynamic-slice_convert_fusion.10), channel_id=1, source_target_pairs={{0,0},{1,4},{2,8},{3,12},{4,16},{5,20},{6,24},{7,28},{8,1},{9,5},{... | collective-permute-start | bytes 110600 | tf_op jit(solution)/shard_map/ppermute | solution.py:413
  17.2 27.4 %collective-permute-start.1 = (bf16[1,520,768]{2,1,0:T(8,128)(2,1)S(1)}, bf16[1,520,768]{2,1,0:T(8,128)(2,1)S(1)}, u32[]{:S(2)}, u32[]{:S(2)}) collective-permute-start(bf16[1,520,768]{2,1,0:T(8,128)(2,1)S(1)} %fusion.7), channel_id=1, source_target_pairs={{0,2},{2,0},{4,6},{6,4},{8,10},{10,8},{12,14},{14,12},{16,18},{18,... | collective-permute-start | bytes 2396168 | tf_op jit(solution)/shard_map/ppermute | solution.py:233
  25.4 11.0 %collective-permute-start.4 = (bf16[2,56,768]{2,1,0:T(8,128)(2,1)S(1)}, bf16[2,56,768]{2,1,0:T(8,128)(2,1)S(1)}, u32[]{:S(2)}, u32[]{:S(2)}) collective-permute-start(bf16[2,56,768]{2,1,0:T(8,128)(2,1)S(1)} %dynamic_update_slice.33), channel_id=1, source_target_pairs={{0,8},{2,10},{4,12},{6,14},{8,16},{10,18},{12,20},{14,22},{16,24},... | collective-permute-start | bytes 516104 | tf_op jit(solution)/shard_map/ppermute | solution.py:241
  26.6 15.2 %collective-permute-start.5 = (bf16[2,56,768]{2,1,0:T(8,128)(2,1)S(1)}, bf16[2,56,768]{2,1,0:T(8,128)(2,1)S(1)}, u32[]{:S(2)}, u32[]{:S(2)}) collective-permute-start(bf16[2,56,768]{2,1,0:T(8,128)(2,1)S(1)} %dynamic_update_slice.33), channel_id=1, source_target_pairs={{0,16},{2,18},{4,20},{6,22},{8,24},{10,26},{12,28},{14,30},{16,0},... | collective-permute-start | bytes 516104 | tf_op jit(solution)/shard_map/ppermute | solution.py:241
  31.8 12.7 %collective-permute-start.6 = (bf16[2,56,768]{2,1,0:T(8,128)(2,1)S(1)}, bf16[2,56,768]{2,1,0:T(8,128)(2,1)S(1)}, u32[]{:S(2)}, u32[]{:S(2)}) collective-permute-start(bf16[2,56,768]{2,1,0:T(8,128)(2,1)S(1)} %dynamic_update_slice.33), channel_id=1, source_target_pairs={{0,24},{2,26},{4,28},{6,30},{8,0},{10,2},{12,4},{14,6},{16,8},{18,... | collective-permute-start | bytes 516104 | tf_op jit(solution)/shard_map/ppermute | solution.py:241
  31.8 16.2 %collective-permute-start.7 = (bf16[2,56,768]{2,1,0:T(8,128)(2,1)S(1)}, bf16[2,56,768]{2,1,0:T(8,128)(2,1)}, u32[]{:S(2)}, u32[]{:S(2)}) collective-permute-start(bf16[2,56,768]{2,1,0:T(8,128)(2,1)S(1)} %dynamic_update_slice.33), channel_id=1, source_target_pairs={{0,4},{2,6},{4,0},{6,2},{8,12},{10,14},{12,8},{14,10},{16,20},{18,... | collective-permute-start | bytes 516104 | tf_op jit(solution)/shard_map/ppermute | solution.py:237
  36.4 12.5 %collective-permute-start.8 = (bf16[2,56,768]{2,1,0:T(8,128)(2,1)S(1)}, bf16[2,56,768]{2,1,0:T(8,128)(2,1)S(1)}, u32[]{:S(2)}, u32[]{:S(2)}) collective-permute-start(bf16[2,56,768]{2,1,0:T(8,128)(2,1)S(1)} %collective-permute-done.4), channel_id=1, source_target_pairs={{0,4},{2,6},{4,0},{6,2},{8,12},{10,14},{12,8},{14,10},{16,20},{18,... | collective-permute-start | bytes 516104 | tf_op jit(solution)/shard_map/ppermute | solution.py:237
  41.8 8.4 %collective-permute-start.9 = (bf16[2,56,768]{2,1,0:T(8,128)(2,1)S(1)}, bf16[2,56,768]{2,1,0:T(8,128)(2,1)S(1)}, u32[]{:S(2)}, u32[]{:S(2)}) collective-permute-start(bf16[2,56,768]{2,1,0:T(8,128)(2,1)S(1)} %collective-permute-done.5), channel_id=1, source_target_pairs={{0,4},{2,6},{4,0},{6,2},{8,12},{10,14},{12,8},{14,10},{16,20},{18,... | collective-permute-start | bytes 516104 | tf_op jit(solution)/shard_map/ppermute | solution.py:237
  44.5 8.7 %collective-permute-start.10 = (bf16[2,56,768]{2,1,0:T(8,128)(2,1)S(1)}, bf16[2,56,768]{2,1,0:T(8,128)(2,1)S(1)}, u32[]{:S(2)}, u32[]{:S(2)}) collective-permute-start(bf16[2,56,768]{2,1,0:T(8,128)(2,1)S(1)} %collective-permute-done.6), channel_id=1, source_target_pairs={{0,4},{2,6},{4,0},{6,2},{8,12},{10,14},{12,8},{14,10},{16,20},{18,... | collective-permute-start | bytes 516104 | tf_op jit(solution)/shard_map/ppermute | solution.py:237
  48.0 8.8 %collective-permute-start.2 = (bf16[2,1,520,768]{3,2,1,0:T(8,128)(2,1)S(1)}, bf16[2,1,520,768]{3,2,1,0:T(8,128)(2,1)}, u32[]{:S(2)}, u32[]{:S(2)}) collective-permute-start(bf16[2,1,520,768]{3,2,1,0:T(8,128)(2,1)S(1)} %get-tuple-element.78), channel_id=1, source_target_pairs={{0,1},{1,0},{2,3},{3,2},{4,5},{5,4},{6,7},{7,6},{8,9},{9,8},{10,11... | collective-permute-start | bytes 4792328 | tf_op jit(solution)/shard_map/ppermute | solution.py:252
  90.2 15.0 %collective-permute-start.13 = (bf16[4,96,768]{2,1,0:T(8,128)(2,1)}, bf16[4,96,768]{2,1,0:T(8,128)(2,1)}, u32[]{:S(2)}, u32[]{:S(2)}) collective-permute-start(bf16[4,96,768]{2,1,0:T(8,128)(2,1)} %fusion.23), channel_id=1, source_target_pairs={{0,4},{2,6},{4,0},{6,2},{8,12},{10,14},{12,8},{14,10},{16,20},{18,... | collective-permute-start | bytes 1769480 | tf_op jit(solution)/shard_map/ppermute | solution.py:237
  106.6 10.5 %collective-permute-start.18 = (bf16[96,768]{1,0:T(8,128)(2,1)S(1)}, bf16[96,768]{1,0:T(8,128)(2,1)S(1)}, u32[]{:S(2)}, u32[]{:S(2)}) collective-permute-start(bf16[96,768]{1,0:T(8,128)(2,1)S(1)} %get-tuple-element.88), channel_id=1, source_target_pairs={{0,24},{2,26},{4,28},{6,30},{8,0},{10,2},{12,4},{14,6},{16,8},{18,... | collective-permute-start | bytes 442376 | tf_op jit(solution)/shard_map/ppermute | solution.py:241
  110.1 17.7 %collective-permute-start.17 = (bf16[96,768]{1,0:T(8,128)(2,1)S(1)}, bf16[96,768]{1,0:T(8,128)(2,1)S(1)}, u32[]{:S(2)}, u32[]{:S(2)}) collective-permute-start(bf16[96,768]{1,0:T(8,128)(2,1)S(1)} %get-tuple-element.89), channel_id=1, source_target_pairs={{0,16},{2,18},{4,20},{6,22},{8,24},{10,26},{12,28},{14,30},{16,0},... | collective-permute-start | bytes 442376 | tf_op jit(solution)/shard_map/ppermute | solution.py:241
  114.9 12.9 %collective-permute-start.16 = (bf16[96,768]{1,0:T(8,128)(2,1)S(1)}, bf16[96,768]{1,0:T(8,128)(2,1)S(1)}, u32[]{:S(2)}, u32[]{:S(2)}) collective-permute-start(bf16[96,768]{1,0:T(8,128)(2,1)S(1)} %get-tuple-element.87), channel_id=1, source_target_pairs={{0,8},{2,10},{4,12},{6,14},{8,16},{10,18},{12,20},{14,22},{16,24},... | collective-permute-start | bytes 442376 | tf_op jit(solution)/shard_map/ppermute | solution.py:241
  152.1 32.1 %collective-permute-start.11 = (bf16[2,1,256,768]{3,2,1,0:T(8,128)(2,1)}, bf16[2,1,256,768]{3,2,1,0:T(8,128)(2,1)}, u32[]{:S(2)}, u32[]{:S(2)}) collective-permute-start(bf16[2,1,256,768]{3,2,1,0:T(8,128)(2,1)} %bitcast.36), channel_id=1, source_target_pairs={{0,1},{1,0},{2,3},{3,2},{4,5},{5,4},{6,7},{7,6},{8,9},{9,8},{10,11... | collective-permute-start | bytes 2359304 | tf_op jit(solution)/shard_map/ppermute | solution.py:252
  152.1 34.5 %collective-permute-start.14 = (bf16[2,1,256,768]{3,2,1,0:T(8,128)(2,1)}, bf16[2,1,256,768]{3,2,1,0:T(8,128)(2,1)}, u32[]{:S(2)}, u32[]{:S(2)}) collective-permute-start(bf16[2,1,256,768]{3,2,1,0:T(8,128)(2,1)} %bitcast.50), channel_id=1, source_target_pairs={{0,1},{1,0},{2,3},{3,2},{4,5},{5,4},{6,7},{7,6},{8,9},{9,8},{10,11... | collective-permute-start | bytes 2359304 | tf_op jit(solution)/shard_map/ppermute | solution.py:252
  153.7 15.6 %collective-permute-start.30 = (bf16[4,96,768]{2,1,0:T(8,128)(2,1)}, bf16[4,96,768]{2,1,0:T(8,128)(2,1)}, u32[]{:S(2)}, u32[]{:S(2)}) collective-permute-start(bf16[4,96,768]{2,1,0:T(8,128)(2,1)} %dynamic-slice_bitcast_fusion), channel_id=1, source_target_pairs={{0,4},{2,6},{4,0},{6,2},{8,12},{10,14},{12,8},{14,10},{16,20},{18,... | collective-permute-start | bytes 1769480 | tf_op jit(solution)/shard_map/ppermute | solution.py:237
  170.5 6.4 %collective-permute-start.33 = (bf16[96,768]{1,0:T(8,128)(2,1)S(1)}, bf16[96,768]{1,0:T(8,128)(2,1)S(1)}, u32[]{:S(2)}, u32[]{:S(2)}) collective-permute-start(bf16[96,768]{1,0:T(8,128)(2,1)S(1)} %get-tuple-element.85), channel_id=1, source_target_pairs={{0,24},{2,26},{4,28},{6,30},{8,0},{10,2},{12,4},{14,6},{16,8},{18,... | collective-permute-start | bytes 442376 | tf_op jit(solution)/shard_map/ppermute | solution.py:241
  170.5 12.6 %collective-permute-start.32 = (bf16[96,768]{1,0:T(8,128)(2,1)S(1)}, bf16[96,768]{1,0:T(8,128)(2,1)S(1)}, u32[]{:S(2)}, u32[]{:S(2)}) collective-permute-start(bf16[96,768]{1,0:T(8,128)(2,1)S(1)} %get-tuple-element.86), channel_id=1, source_target_pairs={{0,16},{2,18},{4,20},{6,22},{8,24},{10,26},{12,28},{14,30},{16,0},... | collective-permute-start | bytes 442376 | tf_op jit(solution)/shard_map/ppermute | solution.py:241
  170.6 12.8 %collective-permute-start.31 = (bf16[96,768]{1,0:T(8,128)(2,1)S(1)}, bf16[96,768]{1,0:T(8,128)(2,1)S(1)}, u32[]{:S(2)}, u32[]{:S(2)}) collective-permute-start(bf16[96,768]{1,0:T(8,128)(2,1)S(1)} %get-tuple-element.84), channel_id=1, source_target_pairs={{0,8},{2,10},{4,12},{6,14},{8,16},{10,18},{12,20},{14,22},{16,24},... | collective-permute-start | bytes 442376 | tf_op jit(solution)/shard_map/ppermute | solution.py:241
  176.9 13.8 %collective-permute-start.19 = (bf16[2,2,56,768]{3,2,1,0:T(8,128)(2,1)S(1)}, bf16[2,2,56,768]{3,2,1,0:T(8,128)(2,1)S(1)}, u32[]{:S(2)}, u32[]{:S(2)}) collective-permute-start(bf16[2,2,56,768]{3,2,1,0:T(8,128)(2,1)S(1)} %pad_maximum_fusion.3), channel_id=1, source_target_pairs={{0,4},{2,6},{4,0},{6,2},{8,12},{10,14},{12,8},{14,10},{16,20},{18,... | collective-permute-start | bytes 1032200 | tf_op jit(solution)/shard_map/ppermute | solution.py:237
  183.1 9.4 %collective-permute-start.20 = (bf16[2,2,56,768]{3,2,1,0:T(8,128)(2,1)S(1)}, bf16[2,2,56,768]{3,2,1,0:T(8,128)(2,1)S(1)}, u32[]{:S(2)}, u32[]{:S(2)}) collective-permute-start(bf16[2,2,56,768]{3,2,1,0:T(8,128)(2,1)S(1)} %pad_maximum_fusion.4), channel_id=1, source_target_pairs={{0,4},{2,6},{4,0},{6,2},{8,12},{10,14},{12,8},{14,10},{16,20},{18,... | collective-permute-start | bytes 1032200 | tf_op jit(solution)/shard_map/ppermute | solution.py:237
  184.2 29.1 %collective-permute-start.34 = (bf16[96,768]{1,0:T(8,128)(2,1)}, bf16[96,768]{1,0:T(8,128)(2,1)}, u32[]{:S(2)}, u32[]{:S(2)}) collective-permute-start(bf16[96,768]{1,0:T(8,128)(2,1)} %fusion.39), channel_id=1, source_target_pairs={{0,1},{1,0},{2,3},{3,2},{4,5},{5,4},{6,7},{7,6},{8,9},{9,8},{10,11... | collective-permute-start | bytes 442376 | tf_op jit(solution)/shard_map/ppermute | solution.py:252
  186.5 46.3 %collective-permute-start.12 = (bf16[1,256,768]{2,1,0:T(8,128)(2,1)}, bf16[1,256,768]{2,1,0:T(8,128)(2,1)}, u32[]{:S(2)}, u32[]{:S(2)}) collective-permute-start(bf16[1,256,768]{2,1,0:T(8,128)(2,1)} %fusion.27), channel_id=1, source_target_pairs={{0,2},{2,0},{4,6},{6,4},{8,10},{10,8},{12,14},{14,12},{16,18},{18,... | collective-permute-start | bytes 1179656 | tf_op jit(solution)/shard_map/ppermute | solution.py:233
  188.6 42.1 %collective-permute-start.15 = (bf16[1,256,768]{2,1,0:T(8,128)(2,1)}, bf16[1,256,768]{2,1,0:T(8,128)(2,1)S(1)}, u32[]{:S(2)}, u32[]{:S(2)}) collective-permute-start(bf16[1,256,768]{2,1,0:T(8,128)(2,1)} %fusion.28), channel_id=1, source_target_pairs={{0,2},{2,0},{4,6},{6,4},{8,10},{10,8},{12,14},{14,12},{16,18},{18,... | collective-permute-start | bytes 1179656 | tf_op jit(solution)/shard_map/ppermute | solution.py:233
  193.9 14.2 %collective-permute-start.21 = (bf16[48,576]{1,0:T(8,128)(2,1)}, bf16[48,576]{1,0:T(8,128)(2,1)}, u32[]{:S(2)}, u32[]{:S(2)}) collective-permute-start(bf16[48,576]{1,0:T(8,128)(2,1)} %fusion.69), channel_id=1, source_target_pairs={{0,2},{2,0},{4,6},{6,4},{8,10},{10,8},{12,14},{14,12},{16,18},{18,... | collective-permute-start | bytes 165896 | tf_op jit(solution)/shard_map/ppermute | solution.py:233
  196.9 26.7 %collective-permute-start.27 = (bf16[2,56,768]{2,1,0:T(8,128)(2,1)}, bf16[2,56,768]{2,1,0:T(8,128)(2,1)}, u32[]{:S(2)}, u32[]{:S(2)}) collective-permute-start(bf16[2,56,768]{2,1,0:T(8,128)(2,1)} %get-tuple-element.79), channel_id=1, source_target_pairs={{0,24},{2,26},{4,28},{6,30},{8,0},{10,2},{12,4},{14,6},{16,8},{18,... | collective-permute-start | bytes 516104 | tf_op jit(solution)/shard_map/ppermute | solution.py:241
  209.3 14.2 %collective-permute-start.26 = (bf16[2,56,768]{2,1,0:T(8,128)(2,1)}, bf16[2,56,768]{2,1,0:T(8,128)(2,1)S(1)}, u32[]{:S(2)}, u32[]{:S(2)}) collective-permute-start(bf16[2,56,768]{2,1,0:T(8,128)(2,1)} %get-tuple-element.76), channel_id=1, source_target_pairs={{0,16},{2,18},{4,20},{6,22},{8,24},{10,26},{12,28},{14,30},{16,0},... | collective-permute-start | bytes 516104 | tf_op jit(solution)/shard_map/ppermute | solution.py:241
  215.9 8.9 %collective-permute-start.25 = (bf16[2,56,768]{2,1,0:T(8,128)(2,1)}, bf16[2,56,768]{2,1,0:T(8,128)(2,1)}, u32[]{:S(2)}, u32[]{:S(2)}) collective-permute-start(bf16[2,56,768]{2,1,0:T(8,128)(2,1)} %get-tuple-element.75), channel_id=1, source_target_pairs={{0,8},{2,10},{4,12},{6,14},{8,16},{10,18},{12,20},{14,22},{16,24},... | collective-permute-start | bytes 516104 | tf_op jit(solution)/shard_map/ppermute | solution.py:241
  230.6 4.6 %collective-permute-start.29 = (bf16[2,56,768]{2,1,0:T(8,128)(2,1)S(1)}, bf16[2,56,768]{2,1,0:T(8,128)(2,1)S(1)}, u32[]{:S(2)}, u32[]{:S(2)}) collective-permute-start(bf16[2,56,768]{2,1,0:T(8,128)(2,1)S(1)} %pad_maximum_fusion.10), channel_id=1, source_target_pairs={{0,1},{1,0},{2,3},{3,2},{4,5},{5,4},{6,7},{7,6},{8,9},{9,8},{10,11... | collective-permute-start | bytes 516104 | tf_op jit(solution)/shard_map/ppermute | solution.py:252
  (57 other events, 310.1 us)
Sparse Core Ops, SparseCore 0:
  33.7 51.3 all-gather.2
